TPU v7x, 32 devices: a whole 2x2x4 slice. The times are simulated.
32 devices in a mesh: ex: 8 (over y, x, core), fsdp: 4 (over z).
Axes of the slice: x: 2, y: 2, z: 4, core: 2. Of those that a mesh axis runs over, the one named last changes fastest.
Arguments:
- tokens: bfloat16 [4096, 4096], P(('ex', 'fsdp')), may hold values from -6 to 6
- cotangent: bfloat16 [4096, 4096], P(('ex', 'fsdp')), may hold values from -6 to 6
- gate_weight: bfloat16 [4096, 14336], P('ex', 'fsdp'), may hold values from -0.09375 to 0.09375
- up_weight: bfloat16 [4096, 14336], P('ex', 'fsdp'), may hold values from -0.09375 to 0.09375
- down_weight: bfloat16 [14336, 4096], P('fsdp', 'ex'), may hold values from -0.046875 to 0.046875
- model_proj: bfloat16 [4096, 128], replicated, may hold values from -0.09375 to 0.09375
- hidden_proj: bfloat16 [14336, 384], P('fsdp'), may hold values from -0.046875 to 0.046875
Outputs:
- features: float32 [8, 8192], P('ex', 'fsdp')
- gram: float32 [8192, 8192], P('fsdp', 'ex')
All inputs are finite; a program needn't handle non-finite values.
Results may differ from a plain program's by a relative error of at most 0.0041.
Values may be sent and summed in bfloat16 or wider, within the bound.
A program may use at most 192 MiB of HBM per device.

v0:
```python
import functools
import math

import jax
import jax.numpy as jnp
from jax import lax
from jax.experimental import pallas as pl
from jax.experimental.pallas import tpu as pltpu
from jax.sharding import PartitionSpec as P


KA = 64
KB = 128
SEQ = 512
F32 = jnp.float32
VMEM_BYTES = 60 * 1024 * 1024


def swap(value, bit, size):
    return lax.ppermute(value, "ex", [(i, i ^ bit) for i in range(size)])


def spread(own, crossed, top, size):
    held = [(0, own), (top, crossed)]
    bit = top // 2
    while bit >= 1:
        more = [(mask | bit, swap(block, bit, size)) for mask, block in held]
        held = held + more
        bit //= 2
    return held


def tile_of(half):
    return 256 if half % 256 == 0 else half


def up_kernel(masks, width, place_ref, x_ref, *refs):
    *blocks, out_ref = refs
    total = None
    for mask, block in zip(masks, blocks):
        start = pl.multiple_of((place_ref[0] ^ mask) * width, width)
        piece = jnp.dot(x_ref[:, pl.ds(start, width)], block[...], preferred_element_type=F32)
        total = piece if total is None else total + piece
    out_ref[...] = total


def up_product(rows, held, place):
    half = held[0][1].shape[1]
    width = held[0][1].shape[0]
    tile = tile_of(half)
    masks = tuple(m for m, _ in held)
    return pl.pallas_call(
        functools.partial(up_kernel, masks, width),
        out_shape=jax.ShapeDtypeStruct((rows.shape[0], half), F32),
        grid_spec=pltpu.PrefetchScalarGridSpec(
            num_scalar_prefetch=1,
            grid=(half // tile,),
            in_specs=[pl.BlockSpec(rows.shape, lambda t, p: (0, 0))]
            + [pl.BlockSpec((width, tile), lambda t, p: (0, t)) for _ in held],
            out_specs=pl.BlockSpec((rows.shape[0], tile), lambda t, p: (0, t)),
        ),
        compiler_params=pltpu.CompilerParams(vmem_limit_bytes=VMEM_BYTES),
    )(place, rows, *[b for _, b in held])


def down_kernel(masks, width, place_ref, y_ref, gate_ref, up_ref, proj_ref, *refs):
    *blocks, b_ref, g_ref = refs
    grad = None
    for mask, block in zip(masks, blocks):
        start = pl.multiple_of((place_ref[0] ^ mask) * width, width)
        piece = lax.dot_general(
            y_ref[:, pl.ds(start, width)], block[...], (((1,), (1,)), ((), ())),
            preferred_element_type=F32,
        )
        grad = piece if grad is None else grad + piece
    gate = gate_ref[...]
    up = up_ref[...]
    sig = jax.nn.sigmoid(gate)
    active = gate * sig
    hidden = (active * up).astype(jnp.bfloat16)
    d_gate = (grad * up * sig * (1.0 + gate * (1.0 - sig))).astype(jnp.bfloat16)
    d_up = (grad * active).astype(jnp.bfloat16)
    b = jnp.dot(hidden, proj_ref[:, :KB], preferred_element_type=F32)
    g = jnp.dot(d_gate, proj_ref[:, KB : 2 * KB], preferred_element_type=F32)
    g = g + jnp.dot(d_up, proj_ref[:, 2 * KB :], preferred_element_type=F32)

    @pl.when(pl.program_id(0) == 0)
    def _():
        b_ref[...] = b
        g_ref[...] = g

    @pl.when(pl.program_id(0) > 0)
    def _():
        b_ref[...] += b
        g_ref[...] += g


def down_product(rows, gate, up, proj, held, place):
    half = held[0][1].shape[0]
    width = held[0][1].shape[1]
    tile = tile_of(half)
    masks = tuple(m for m, _ in held)
    count = rows.shape[0]
    return pl.pallas_call(
        functools.partial(down_kernel, masks, width),
        out_shape=[jax.ShapeDtypeStruct((count, KB), F32)] * 2,
        grid_spec=pltpu.PrefetchScalarGridSpec(
            num_scalar_prefetch=1,
            grid=(half // tile,),
            in_specs=[
                pl.BlockSpec(rows.shape, lambda t, p: (0, 0)),
                pl.BlockSpec((count, tile), lambda t, p: (0, t)),
                pl.BlockSpec((count, tile), lambda t, p: (0, t)),
                pl.BlockSpec((tile, proj.shape[1]), lambda t, p: (t, 0)),
            ]
            + [pl.BlockSpec((tile, width), lambda t, p: (t, 0)) for _ in held],
            out_specs=[pl.BlockSpec((count, KB), lambda t, p: (0, 0))] * 2,
        ),
        compiler_params=pltpu.CompilerParams(vmem_limit_bytes=VMEM_BYTES),
    )(place, rows, gate, up, proj, *[b for _, b in held])


def share_kernel(
    size, deep, part_ref, left_ref, right_ref, got, own, send1, recv1, send_a, send_b, left_sem, right_sem
):
    top = size // 2
    group = 2 * deep
    per = group // size
    ex = lax.axis_index("ex")
    z = lax.axis_index("fsdp")
    side = ex // top
    base = ex % top
    me = side * deep + z

    def to(src, dst, ss, rs, dev_ex, dev_z):
        return pltpu.make_async_remote_copy(
            src_ref=src, dst_ref=dst, send_sem=ss, recv_sem=rs,
            device_id={"ex": dev_ex, "fsdp": dev_z},
            device_id_type=pl.DeviceIdType.MESH,
        )

    def first(q, rs):
        return to(
            part_ref.at[q], got.at[me], send1.at[q], rs, (q // deep) * top + base, q % deep
        )

    for k in range(1, group):
        q = (me + k) % group
        first(q, recv1.at[me]).start()
    total = part_ref[me]
    for k in range(1, group):
        q = (me + k) % group
        to(part_ref.at[q], got.at[q], send1.at[q], recv1.at[q], ex, z).wait_recv()
        total = total + got[q]
    own[...] = total

    row_z = me // 2
    col_ex = me // per
    half = me % 2
    slot = me % per

    def row_copy(k):
        return to(own, left_ref.at[base, half], send_a.at[k], left_sem.at[base, half], (ex + k) % size, row_z)

    def col_copy(k):
        return to(own, right_ref.at[base, slot], send_b.at[k], right_sem.at[base, slot], col_ex, (z + k) % deep)

    for k in range(size):
        if k == 0:
            @pl.when(row_z != z)
            def _():
                row_copy(0).start()
        else:
            row_copy(k).start()
    for k in range(deep):
        if k == 0:
            @pl.when(col_ex != ex)
            def _():
                col_copy(0).start()
        else:
            col_copy(k).start()

    @pl.when(row_z == z)
    def _():
        left_ref[base, half] = total

    @pl.when(col_ex == ex)
    def _():
        right_ref[base, slot] = total

    for b in range(top):
        for h in range(2):
            q = 2 * z + h

            @pl.when(jnp.logical_or(b != base, q != me))
            def _():
                to(own, left_ref.at[b, h], send_a.at[0], left_sem.at[b, h], ex, z).wait_recv()

        for r in range(per):
            q = ex * per + r

            @pl.when(jnp.logical_or(b != base, q != me))
            def _():
                to(own, right_ref.at[b, r], send_b.at[0], right_sem.at[b, r], ex, z).wait_recv()

    for k in range(1, group):
        first((me + k) % group, recv1.at[me]).wait_send()
    for k in range(size):
        if k == 0:
            @pl.when(row_z != z)
            def _():
                row_copy(0).wait_send()
        else:
            row_copy(k).wait_send()
    for k in range(deep):
        if k == 0:
            @pl.when(col_ex != ex)
            def _():
                col_copy(0).wait_send()
        else:
            col_copy(k).wait_send()


def share(part, size, deep):
    group, two, chunk = part.shape
    top = size // 2
    per = group // size
    dma = pltpu.SemaphoreType.DMA
    return pl.pallas_call(
        functools.partial(share_kernel, size, deep),
        out_shape=[
            jax.ShapeDtypeStruct((top, 2, two, chunk), F32),
            jax.ShapeDtypeStruct((top, per, two, chunk), F32),
        ],
        in_specs=[pl.BlockSpec(memory_space=pltpu.VMEM)],
        out_specs=[pl.BlockSpec(memory_space=pltpu.VMEM)] * 2,
        scratch_shapes=[
            pltpu.VMEM((group, two, chunk), F32),
            pltpu.VMEM((two, chunk), F32),
            dma((group,)), dma((group,)), dma((size,)), dma((deep,)),
            dma((top, 2)), dma((top, per)),
        ],
        compiler_params=pltpu.CompilerParams(has_side_effects=True),
    )(part)


def pair_product(left, right, count):
    left_three = left.reshape(count, SEQ, left.shape[1])
    right_three = right.reshape(count, SEQ, right.shape[1])
    return jnp.einsum("esi,esj->eij", left_three, right_three, precision=lax.Precision.HIGHEST)


def body(tokens, cotangent, gate_weight, up_weight, down_weight, model_proj, hidden_proj):
    size = lax.axis_size("ex")
    deep = lax.axis_size("fsdp")
    top = size // 2
    place = lax.axis_index("ex")
    side = place // top
    half = gate_weight.shape[1] // 2

    def halves(weight, axis):
        mine = lax.dynamic_slice_in_dim(weight, side * half, half, axis)
        theirs = lax.dynamic_slice_in_dim(weight, (1 - side) * half, half, axis)
        return mine, theirs

    gate_mine, gate_theirs = halves(gate_weight, 1)
    up_mine, up_theirs = halves(up_weight, 1)
    down_mine, down_theirs = halves(down_weight, 0)

    in_own = lax.all_gather(tokens, "fsdp", axis=0, tiled=True)
    cot_pair = jnp.concatenate([cotangent, swap(cotangent, top, size)], axis=1)
    cot_both = lax.all_gather(cot_pair, "fsdp", axis=0, tiled=True)
    dim = in_own.shape[1]
    whole_in = jnp.concatenate([in_own, swap(in_own, top, size)], axis=0)
    whole_cot = jnp.concatenate([cot_both[:, :dim], cot_both[:, dim:]], axis=0)

    gates = spread(gate_mine, swap(gate_theirs, top, size), top, size)
    ups = spread(up_mine, swap(up_theirs, top, size), top, size)
    downs = spread(down_mine, swap(down_theirs, top, size), top, size)

    where = place.astype(jnp.int32).reshape(1)
    gate = up_product(whole_in, gates, where)
    up = up_product(whole_in, ups, where)
    proj_in = jnp.dot(whole_in, model_proj[:, :KA], preferred_element_type=F32)
    proj_cot = jnp.dot(whole_cot, model_proj[:, KA:], preferred_element_type=F32)
    hp = lax.dynamic_slice_in_dim(hidden_proj, side * half, half, 0)
    proj_hidden, proj_grad = down_product(whole_cot, gate, up, hp, downs, where)
    part = pair_product(proj_in, proj_grad, 2) + pair_product(proj_cot, proj_hidden, 2)
    part = (part * (1.0 / math.sqrt(SEQ))).reshape(2, KA * KB)
    part = jnp.where(side == 0, part, part[::-1])
    chunk = KA * KB // (2 * deep)
    part = part.reshape(2, 2 * deep, chunk).transpose(1, 0, 2)
    left, right = share(part, size, deep)
    left = left.transpose(2, 0, 1, 3).reshape(size, 2 * chunk)
    right = right.transpose(2, 0, 1, 3).reshape(size, -1)
    features = lax.dynamic_slice_in_dim(left, place, 1, 0)
    gram = jnp.dot(left.T, right, precision=lax.Precision.HIGHEST) / size
    return (features, gram)


def solution(mesh):
    placed = (
        P(("ex", "fsdp"), None),
        P(("ex", "fsdp"), None),
        P("ex", "fsdp"),
        P("ex", "fsdp"),
        P("fsdp", "ex"),
        P(),
        P("fsdp", None),
    )
    return jax.shard_map(
        body,
        mesh=mesh,
        in_specs=placed,
        out_specs=(P("ex", "fsdp"), P("fsdp", "ex")),
        check_vma=False,
    )
```

profile of v0, /device:TPU:0, one launch (start us, length us, event | category | flops | bytes accessed | tf_op | source)
XLA Modules:
  0.0 493.2 jit_solution(1551611514544177351)
XLA Ops:
  7.2 0.0 copy-start
  7.2 0.0 all-gather.3.cloned.1.call-start
  7.2 0.7 all-gather.3.cloned.1.call-update
  7.9 0.0 all-gather.5.cloned.1.call-start
  8.0 3.1 collective-permute-start.1
  11.0 23.4 %collective-permute-done.1 = bf16[128,4096]{1,0:T(8,128)(2,1)S(1)} collective-permute-done((bf16[128,4096]{1,0:T(8,128)(2,1)}, bf16[128,4096]{1,0:T(8,128)(2,1)S(1)}, u32[]{:S(2)}, u32[]{:S(2)}) %collective-permute-start.1) | collective-permute-done | bytes 1048608 | tf_op jit(solution)/shard_map/ppermute | solution.py:20
  34.4 2.8 pad_maximum_fusion.1
  37.2 0.0 all-gather.5.cloned.1.call-update
  37.3 0.0 copy-start.5
  37.3 4.3 constant_dynamic-slice_fusion.4
  41.6 1.7 collective-permute-start.10
  43.3 0.0 collective-permute-start.12
  43.3 1.5 collective-permute-start.9
  44.8 2.1 constant_dynamic-slice_fusion.6
  46.9 0.5 collective-permute-start.2
  47.4 45.6 %all-gather.3.cloned.1.call-done = bf16[512,4096]{1,0:T(8,128)(2,1)} async-done(((bf16[128,4096]{1,0:T(8,128)(2,1)}), bf16[512,4096]{1,0:T(8,128)(2,1)}) %all-gather.3.cloned.1.call-update) | async-done | bytes 4194320 | tf_op jit(solution)/shard_map/all_gather | solution.py:270
  93.1 1.5 collective-permute-start
  94.5 3.5 constant_dynamic-slice_fusion.1
  98.1 1.5 collective-permute-start.3
  99.6 0.6 collective-permute-start.16
  100.2 25.7 %collective-permute-done.2.refs_1_ = bf16[512,1792]{1,0:T(8,128)(2,1)} collective-permute-done((bf16[512,1792]{1,0:T(8,128)(2,1)}, bf16[512,1792]{1,0:T(8,128)(2,1)}, u32[]{:S(2)}, u32[]{:S(2)}) %collective-permute-start.2) | collective-permute-done | bytes 1835040 | tf_op jit(solution)/shard_map/ppermute | solution.py:20
  125.8 0.3 collective-permute-start.11
  126.2 14.9 %collective-permute-done.3.refs_2_ = bf16[512,1792]{1,0:T(8,128)(2,1)} collective-permute-done((bf16[512,1792]{1,0:T(8,128)(2,1)S(1)}, bf16[512,1792]{1,0:T(8,128)(2,1)}, u32[]{:S(2)}, u32[]{:S(2)}) %collective-permute-start.3) | collective-permute-done | bytes 1835040 | tf_op jit(solution)/shard_map/ppermute | solution.py:20
  141.1 1.3 copy-done.6
  142.4 0.5 collective-permute-start.14
  142.9 111.7 %collective-permute-done.16.refs_1_ = bf16[1792,512]{1,0:T(8,128)(2,1)} collective-permute-done((bf16[1792,512]{1,0:T(8,128)(2,1)S(1)}, bf16[1792,512]{1,0:T(8,128)(2,1)}, u32[]{:S(2)}, u32[]{:S(2)}) %collective-permute-start.16) | collective-permute-done | bytes 1835040 | tf_op jit(solution)/shard_map/ppermute | solution.py:20
  254.6 0.3 collective-permute-start.4
  254.9 1.3 copy-done.7
  256.2 1.8 collective-permute-start.17
  258.0 0.2 collective-permute-start.6
  258.1 39.7 %collective-permute-done.4.refs_3_ = bf16[512,1792]{1,0:T(8,128)(2,1)} collective-permute-done((bf16[512,1792]{1,0:T(8,128)(2,1)}, bf16[512,1792]{1,0:T(8,128)(2,1)}, u32[]{:S(2)}, u32[]{:S(2)}) %collective-permute-start.4) | collective-permute-done | bytes 1835040 | tf_op jit(solution)/shard_map/ppermute | solution.py:20
  297.8 0.4 collective-permute-start.18
  298.2 0.8 copy-done.10
  299.0 0.5 collective-permute-start.8
  299.5 1.2 constant_dynamic-slice_fusion.3.proj_ref
  300.7 4.7 constant_dynamic-update-slice_fusion.1
  305.4 4.7 constant_dynamic-update-slice_fusion.x_ref
  310.1 22.1 %shard_map.87.up_ref = f32[1024,1792]{1,0:T(8,128)} custom-call(s32[1]{0:T(128)} %bitcast.place_ref, bf16[1024,4096]{1,0:T(8,128)(2,1)} %constant_dynamic-update-slice_fusion.x_ref, bf16[512,1792]{1,0:T(8,128)(2,1)} %get-tuple-element.15.refs_0_, bf16[512,1792]{1,0:T(8,128)(2,1)} %collective-permute-done.9.refs_1_, ...), custom_call_target="tpu_custom_call" | custom-call | tf_op jit(solution)/shard_map/pallas_call | solution.py:52
  332.2 4.9 collective-permute-done.17.refs_2_
  337.1 0.5 collective-permute-start.20
  337.6 0.1 collective-permute-start.21
  337.7 37.4 %collective-permute-done.18.refs_3_ = bf16[1792,512]{1,0:T(8,128)(2,1)} collective-permute-done((bf16[1792,512]{1,0:T(8,128)(2,1)}, bf16[1792,512]{1,0:T(8,128)(2,1)}, u32[]{:S(2)}, u32[]{:S(2)}) %collective-permute-start.18) | collective-permute-done | bytes 1835040 | tf_op jit(solution)/shard_map/ppermute | solution.py:20
  375.1 22.1 %shard_map.86.gate_ref = f32[1024,1792]{1,0:T(8,128)} custom-call(s32[1]{0:T(128)} %bitcast.place_ref, bf16[1024,4096]{1,0:T(8,128)(2,1)} %constant_dynamic-update-slice_fusion.x_ref, bf16[512,1792]{1,0:T(8,128)(2,1)} %get-tuple-element.17.refs_0_, bf16[512,1792]{1,0:T(8,128)(2,1)} %collective-permute-done.2.refs_1_, ...), custom_call_target="tpu_custom_call" | custom-call | tf_op jit(solution)/shard_map/pallas_call | solution.py:52
  397.2 6.0 %fusion.4 = f32[1024,64]{0,1:T(8,128)S(1)} fusion(bf16[1024,4096]{1,0:T(8,128)(2,1)} %constant_dynamic-update-slice_fusion.x_ref, bf16[4096,128]{1,0:T(8,128)(2,1)S(1)} %copy-done.12), kind=kOutput, calls=%fused_computation.8 | convolution fusion | flops 536870912 | bytes 9699328 | tf_op jit(solution)/shard_map/dot_general | solution.py:284
  403.2 0.0 all-gather.5.cloned.1.call-done
  403.3 0.0 copy-start.13
  403.3 4.0 fusion.11
  407.4 2.0 copy-done.2
  409.4 1.3 copy-done.3
  410.7 2.7 fusion.2
  413.4 8.0 %pad_maximum_fusion.y_ref = bf16[1024,4096]{1,0:T(8,128)(2,1)} fusion(bf16[512,4096]{1,0:T(8,128)(2,1)} %copy-done.3, bf16[512,4096]{1,0:T(8,128)(2,1)} %copy-done.2), kind=kLoop, calls=%fused_computation | loop fusion | flops 16777216 | bytes 16777216 | tf_op jit(solution)/shard_map/concatenate | solution.py:275
  421.4 1.3 copy-done.11
  422.7 30.3 %shard_map.88 = (f32[1024,128]{1,0:T(8,128)}, f32[1024,128]{1,0:T(8,128)}) custom-call(s32[1]{0:T(128)} %bitcast.place_ref, bf16[1024,4096]{1,0:T(8,128)(2,1)} %pad_maximum_fusion.y_ref, f32[1024,1792]{1,0:T(8,128)} %shard_map.86.gate_ref, f32[1024,1792]{1,0:T(8,128)} %shard_map.87.up_ref, bf16[1792,384]{1,0:T(8,128)(2,1)} %constant_dynamic-slice_fusion.3.proj_ref, ...), custom_call_target="tpu_custom_call" | custom-call | tf_op jit(solution)/shard_map/pallas_call | solution.py:104
  453.0 1.5 fusion.6
  454.5 1.5 fusion.1
  455.9 0.1 copy.30
  456.0 1.6 rev.3
  457.6 0.7 broadcast_select_fusion
  458.3 16.8 %shard_map.89 = (f32[4,2,2,1024]{3,2,1,0:T(2,128)}, f32[4,1,2,1024]{3,2,1,0:T(2,128)}) custom-call(f32[8,2,1024]{2,1,0:T(2,128)} %bitcast.38), custom_call_target="tpu_custom_call" | custom-call | tf_op jit(solution)/shard_map/pallas_call | solution.py:229
  475.1 0.9 copy.13
  476.0 0.8 copy.14
  476.8 0.0 copy-start.1
  476.8 9.0 %convolution_multiply_fusion = f32[2048,1024]{1,0:T(8,128)} fusion(f32[8,2048]{1,0:T(8,128)S(1)} %bitcast.34, f32[8,1024]{1,0:T(8,128)S(1)} %reshape.39), kind=kOutput, calls=%fused_computation.1 | convolution fusion | flops 203423744 | bytes 8486912 | tf_op jit(solution)/shard_map/dot_general | solution.py:297
  485.8 0.6 constant_dynamic-slice_fusion
  (42 shorter events, 0.1 us)
Async XLA Ops:
  7.2 292.4 %copy-start = (bf16[3584,384]{1,0:T(8,128)(2,1)S(1)}, bf16[3584,384]{1,0:T(8,128)(2,1)}, u32[]{:S(2)}) copy-start(bf16[3584,384]{1,0:T(8,128)(2,1)} %param.13) | copy-start | bytes 8257540
  7.2 85.9 %all-gather.3.cloned.1.call-start = ((), (), s32[]{:S(2)}) async-start(), calls=%async_computation | async-start | bytes 5242880 | tf_op jit(solution)/shard_map/all_gather | solution.py:270
  7.9 395.4 %all-gather.5.cloned.1.call-start = ((), (), s32[]{:S(2)}) async-start(), calls=%async_computation.1 | async-start | bytes 10485760 | tf_op jit(solution)/shard_map/all_gather | solution.py:272
  8.0 26.4 %collective-permute-start.1 = (bf16[128,4096]{1,0:T(8,128)(2,1)}, bf16[128,4096]{1,0:T(8,128)(2,1)S(1)}, u32[]{:S(2)}, u32[]{:S(2)}) collective-permute-start(bf16[128,4096]{1,0:T(8,128)(2,1)} %param.8), channel_id=1, source_target_pairs={{0,16},{4,20},{8,24},{12,28},{16,0},{20,4},{24,8},{28,12},{1,17},{... | collective-permute-start | bytes 3145736 | tf_op jit(solution)/shard_map/ppermute | solution.py:20
  37.3 7.6 %copy-start.5 = (bf16[512,3584]{1,0:T(8,128)(2,1)S(1)}, bf16[512,3584]{1,0:T(8,128)(2,1)}, u32[]{:S(2)}) copy-start(bf16[512,3584]{1,0:T(8,128)(2,1)} %param.9) | copy-start | bytes 11010052
  41.6 58.0 %collective-permute-start.10 = (bf16[512,1792]{1,0:T(8,128)(2,1)}, bf16[512,1792]{1,0:T(8,128)(2,1)}, u32[]{:S(2)}, u32[]{:S(2)}) collective-permute-start(bf16[512,1792]{1,0:T(8,128)(2,1)} %get-tuple-element.15.refs_0_), channel_id=1, source_target_pairs={{0,8},{4,12},{8,0},{12,4},{16,24},{20,28},{24,16},{28,20},{1,9},{5... | collective-permute-start | bytes 5505032 | tf_op jit(solution)/shard_map/ppermute | solution.py:20
  43.3 56.2 %collective-permute-start.12 = (bf16[512,1792]{1,0:T(8,128)(2,1)}, bf16[512,1792]{1,0:T(8,128)(2,1)}, u32[]{:S(2)}, u32[]{:S(2)}) collective-permute-start(bf16[512,1792]{1,0:T(8,128)(2,1)} %get-tuple-element.15.refs_0_), channel_id=1, source_target_pairs={{0,4},{4,0},{8,12},{12,8},{16,20},{20,16},{24,28},{28,24},{1,5},{5... | collective-permute-start | bytes 5505032 | tf_op jit(solution)/shard_map/ppermute | solution.py:20
  43.3 54.8 %collective-permute-start.9 = (bf16[512,1792]{1,0:T(8,128)(2,1)}, bf16[512,1792]{1,0:T(8,128)(2,1)}, u32[]{:S(2)}, u32[]{:S(2)}) collective-permute-start(bf16[512,1792]{1,0:T(8,128)(2,1)} %get-tuple-element.14), channel_id=1, source_target_pairs={{0,16},{4,20},{8,24},{12,28},{16,0},{20,4},{24,8},{28,12},{1,17},{... | collective-permute-start | bytes 5505032 | tf_op jit(solution)/shard_map/ppermute | solution.py:20
  46.9 78.9 %collective-permute-start.2 = (bf16[512,1792]{1,0:T(8,128)(2,1)}, bf16[512,1792]{1,0:T(8,128)(2,1)}, u32[]{:S(2)}, u32[]{:S(2)}) collective-permute-start(bf16[512,1792]{1,0:T(8,128)(2,1)} %get-tuple-element.16), channel_id=1, source_target_pairs={{0,16},{4,20},{8,24},{12,28},{16,0},{20,4},{24,8},{28,12},{1,17},{... | collective-permute-start | bytes 5505032 | tf_op jit(solution)/shard_map/ppermute | solution.py:20
  93.1 5.0 %copy-start.4 = (bf16[512,1792]{1,0:T(8,128)(2,1)S(1)}, bf16[512,1792]{1,0:T(8,128)(2,1)}, u32[]{:S(2)}) copy-start(bf16[512,1792]{1,0:T(8,128)(2,1)} %get-tuple-element.17.refs_0_) | copy-start | bytes 5505028
  93.1 205.1 %collective-permute-start = (bf16[512,4096]{1,0:T(8,128)(2,1)}, bf16[512,4096]{1,0:T(8,128)(2,1)}, u32[]{:S(2)}, u32[]{:S(2)}) collective-permute-start(bf16[512,4096]{1,0:T(8,128)(2,1)} %all-gather.3.cloned.1.call-done), channel_id=1, source_target_pairs={{0,16},{4,20},{8,24},{12,28},{16,0},{20,4},{24,8},{28,12},{1,17},{... | collective-permute-start | bytes 12582920 | tf_op jit(solution)/shard_map/ppermute | solution.py:20
  98.1 43.0 %collective-permute-start.3 = (bf16[512,1792]{1,0:T(8,128)(2,1)S(1)}, bf16[512,1792]{1,0:T(8,128)(2,1)}, u32[]{:S(2)}, u32[]{:S(2)}) collective-permute-start(bf16[512,1792]{1,0:T(8,128)(2,1)S(1)} %copy-done.4), channel_id=1, source_target_pairs={{0,8},{4,12},{8,0},{12,4},{16,24},{20,28},{24,16},{28,20},{1,9},{5... | collective-permute-start | bytes 5505032 | tf_op jit(solution)/shard_map/ppermute | solution.py:20
  99.6 41.5 %collective-permute-start.5 = (bf16[512,1792]{1,0:T(8,128)(2,1)S(1)}, bf16[512,1792]{1,0:T(8,128)(2,1)S(1)}, u32[]{:S(2)}, u32[]{:S(2)}) collective-permute-start(bf16[512,1792]{1,0:T(8,128)(2,1)S(1)} %copy-done.4), channel_id=1, source_target_pairs={{0,4},{4,0},{8,12},{12,8},{16,20},{20,16},{24,28},{28,24},{1,5},{5... | collective-permute-start | bytes 5505032 | tf_op jit(solution)/shard_map/ppermute | solution.py:20
  99.6 155.0 %collective-permute-start.16 = (bf16[1792,512]{1,0:T(8,128)(2,1)S(1)}, bf16[1792,512]{1,0:T(8,128)(2,1)}, u32[]{:S(2)}, u32[]{:S(2)}) collective-permute-start(bf16[1792,512]{1,0:T(8,128)(2,1)S(1)} %get-tuple-element.12), channel_id=1, source_target_pairs={{0,16},{4,20},{8,24},{12,28},{16,0},{20,4},{24,8},{28,12},{1,17},{... | collective-permute-start | bytes 5505032 | tf_op jit(solution)/shard_map/ppermute | solution.py:20
  125.8 129.1 %collective-permute-start.11 = (bf16[512,1792]{1,0:T(8,128)(2,1)}, bf16[512,1792]{1,0:T(8,128)(2,1)S(1)}, u32[]{:S(2)}, u32[]{:S(2)}) collective-permute-start(bf16[512,1792]{1,0:T(8,128)(2,1)} %collective-permute-done.9.refs_1_), channel_id=1, source_target_pairs={{0,8},{4,12},{8,0},{12,4},{16,24},{20,28},{24,16},{28,20},{1,9},{5... | collective-permute-start | bytes 5505032 | tf_op jit(solution)/shard_map/ppermute | solution.py:20
  141.1 115.1 %collective-permute-start.13 = (bf16[512,1792]{1,0:T(8,128)(2,1)}, bf16[512,1792]{1,0:T(8,128)(2,1)S(1)}, u32[]{:S(2)}, u32[]{:S(2)}) collective-permute-start(bf16[512,1792]{1,0:T(8,128)(2,1)} %collective-permute-done.9.refs_1_), channel_id=1, source_target_pairs={{0,4},{4,0},{8,12},{12,8},{16,20},{20,16},{24,28},{28,24},{1,5},{5... | collective-permute-start | bytes 5505032 | tf_op jit(solution)/shard_map/ppermute | solution.py:20
  141.1 1.3 copy-start.6
  142.4 115.6 %collective-permute-start.14 = (bf16[512,1792]{1,0:T(8,128)(2,1)}, bf16[512,1792]{1,0:T(8,128)(2,1)S(1)}, u32[]{:S(2)}, u32[]{:S(2)}) collective-permute-start(bf16[512,1792]{1,0:T(8,128)(2,1)} %collective-permute-done.10.refs_2_), channel_id=1, source_target_pairs={{0,4},{4,0},{8,12},{12,8},{16,20},{20,16},{24,28},{28,24},{1,5},{5... | collective-permute-start | bytes 5505032 | tf_op jit(solution)/shard_map/ppermute | solution.py:20
  254.6 43.2 %collective-permute-start.4 = (bf16[512,1792]{1,0:T(8,128)(2,1)}, bf16[512,1792]{1,0:T(8,128)(2,1)}, u32[]{:S(2)}, u32[]{:S(2)}) collective-permute-start(bf16[512,1792]{1,0:T(8,128)(2,1)} %collective-permute-done.2.refs_1_), channel_id=1, source_target_pairs={{0,8},{4,12},{8,0},{12,4},{16,24},{20,28},{24,16},{28,20},{1,9},{5... | collective-permute-start | bytes 5505032 | tf_op jit(solution)/shard_map/ppermute | solution.py:20
  254.9 1.3 copy-start.7
  256.2 41.6 %collective-permute-start.15 = (bf16[512,1792]{1,0:T(8,128)(2,1)S(1)}, bf16[512,1792]{1,0:T(8,128)(2,1)S(1)}, u32[]{:S(2)}, u32[]{:S(2)}) collective-permute-start(bf16[512,1792]{1,0:T(8,128)(2,1)S(1)} %collective-permute-done.11.refs_3_), channel_id=1, source_target_pairs={{0,4},{4,0},{8,12},{12,8},{16,20},{20,16},{24,28},{28,24},{1,5},{5... | collective-permute-start | bytes 5505032 | tf_op jit(solution)/shard_map/ppermute | solution.py:20
  256.2 41.6 %copy-start.8 = (bf16[512,1792]{1,0:T(8,128)(2,1)}, bf16[512,1792]{1,0:T(8,128)(2,1)S(1)}, u32[]{:S(2)}) copy-start(bf16[512,1792]{1,0:T(8,128)(2,1)S(1)} %collective-permute-done.13.refs_5_) | copy-start | bytes 5505028
  256.2 80.9 %collective-permute-start.17 = (bf16[1792,512]{1,0:T(8,128)(2,1)}, bf16[1792,512]{1,0:T(8,128)(2,1)}, u32[]{:S(2)}, u32[]{:S(2)}) collective-permute-start(bf16[1792,512]{1,0:T(8,128)(2,1)} %get-tuple-element.13.refs_0_), channel_id=1, source_target_pairs={{0,8},{4,12},{8,0},{12,4},{16,24},{20,28},{24,16},{28,20},{1,9},{5... | collective-permute-start | bytes 5505032 | tf_op jit(solution)/shard_map/ppermute | solution.py:20
  258.0 40.2 %copy-start.9 = (bf16[512,1792]{1,0:T(8,128)(2,1)}, bf16[512,1792]{1,0:T(8,128)(2,1)S(1)}, u32[]{:S(2)}) copy-start(bf16[512,1792]{1,0:T(8,128)(2,1)S(1)} %collective-permute-done.14.refs_6_) | copy-start | bytes 5505028
  258.0 79.2 %collective-permute-start.6 = (bf16[512,1792]{1,0:T(8,128)(2,1)}, bf16[512,1792]{1,0:T(8,128)(2,1)}, u32[]{:S(2)}, u32[]{:S(2)}) collective-permute-start(bf16[512,1792]{1,0:T(8,128)(2,1)} %collective-permute-done.2.refs_1_), channel_id=1, source_target_pairs={{0,4},{4,0},{8,12},{12,8},{16,20},{20,16},{24,28},{28,24},{1,5},{5... | collective-permute-start | bytes 5505032 | tf_op jit(solution)/shard_map/ppermute | solution.py:20
  297.8 39.8 %collective-permute-start.7 = (bf16[512,1792]{1,0:T(8,128)(2,1)}, bf16[512,1792]{1,0:T(8,128)(2,1)}, u32[]{:S(2)}, u32[]{:S(2)}) collective-permute-start(bf16[512,1792]{1,0:T(8,128)(2,1)} %collective-permute-done.3.refs_2_), channel_id=1, source_target_pairs={{0,4},{4,0},{8,12},{12,8},{16,20},{20,16},{24,28},{28,24},{1,5},{5... | collective-permute-start | bytes 5505032 | tf_op jit(solution)/shard_map/ppermute | solution.py:20
  297.8 1.2 copy-start.10
  297.8 77.3 %collective-permute-start.18 = (bf16[1792,512]{1,0:T(8,128)(2,1)}, bf16[1792,512]{1,0:T(8,128)(2,1)}, u32[]{:S(2)}, u32[]{:S(2)}) collective-permute-start(bf16[1792,512]{1,0:T(8,128)(2,1)} %collective-permute-done.16.refs_1_), channel_id=1, source_target_pairs={{0,8},{4,12},{8,0},{12,4},{16,24},{20,28},{24,16},{28,20},{1,9},{5... | collective-permute-start | bytes 5505032 | tf_op jit(solution)/shard_map/ppermute | solution.py:20
  299.0 76.1 %collective-permute-start.8 = (bf16[512,1792]{1,0:T(8,128)(2,1)}, bf16[512,1792]{1,0:T(8,128)(2,1)}, u32[]{:S(2)}, u32[]{:S(2)}) collective-permute-start(bf16[512,1792]{1,0:T(8,128)(2,1)} %collective-permute-done.4.refs_3_), channel_id=1, source_target_pairs={{0,4},{4,0},{8,12},{12,8},{16,20},{20,16},{24,28},{28,24},{1,5},{5... | collective-permute-start | bytes 5505032 | tf_op jit(solution)/shard_map/ppermute | solution.py:20
  332.2 65.0 %copy-start.12 = (bf16[4096,128]{1,0:T(8,128)(2,1)S(1)}, bf16[4096,128]{1,0:T(8,128)(2,1)}, u32[]{:S(2)}) copy-start(bf16[4096,128]{1,0:T(8,128)(2,1)} %param.12) | copy-start | bytes 3145732
  337.1 84.3 %collective-permute-start.19 = (bf16[1792,512]{1,0:T(8,128)(2,1)}, bf16[1792,512]{1,0:T(8,128)(2,1)S(1)}, u32[]{:S(2)}, u32[]{:S(2)}) collective-permute-start(bf16[1792,512]{1,0:T(8,128)(2,1)} %get-tuple-element.13.refs_0_), channel_id=1, source_target_pairs={{0,4},{4,0},{8,12},{12,8},{16,20},{20,16},{24,28},{28,24},{1,5},{5... | collective-permute-start | bytes 5505032 | tf_op jit(solution)/shard_map/ppermute | solution.py:20
  337.1 84.3 %collective-permute-start.20 = (bf16[1792,512]{1,0:T(8,128)(2,1)}, bf16[1792,512]{1,0:T(8,128)(2,1)}, u32[]{:S(2)}, u32[]{:S(2)}) collective-permute-start(bf16[1792,512]{1,0:T(8,128)(2,1)} %collective-permute-done.16.refs_1_), channel_id=1, source_target_pairs={{0,4},{4,0},{8,12},{12,8},{16,20},{20,16},{24,28},{28,24},{1,5},{5... | collective-permute-start | bytes 5505032 | tf_op jit(solution)/shard_map/ppermute | solution.py:20
  337.6 83.8 %collective-permute-start.21 = (bf16[1792,512]{1,0:T(8,128)(2,1)}, bf16[1792,512]{1,0:T(8,128)(2,1)}, u32[]{:S(2)}, u32[]{:S(2)}) collective-permute-start(bf16[1792,512]{1,0:T(8,128)(2,1)} %collective-permute-done.17.refs_2_), channel_id=1, source_target_pairs={{0,4},{4,0},{8,12},{12,8},{16,20},{20,16},{24,28},{28,24},{1,5},{5... | collective-permute-start | bytes 5505032 | tf_op jit(solution)/shard_map/ppermute | solution.py:20
  375.1 46.3 %collective-permute-start.22 = (bf16[1792,512]{1,0:T(8,128)(2,1)}, bf16[1792,512]{1,0:T(8,128)(2,1)}, u32[]{:S(2)}, u32[]{:S(2)}) collective-permute-start(bf16[1792,512]{1,0:T(8,128)(2,1)} %collective-permute-done.18.refs_3_), channel_id=1, source_target_pairs={{0,4},{4,0},{8,12},{12,8},{16,20},{20,16},{24,28},{28,24},{1,5},{5... | collective-permute-start | bytes 5505032 | tf_op jit(solution)/shard_map/ppermute | solution.py:20
  403.3 7.4 %copy-start.13 = (bf16[4096,128]{1,0:T(8,128)(2,1)S(1)}, bf16[4096,128]{1,0:T(8,128)(2,1)}, u32[]{:S(2)}) copy-start(bf16[4096,128]{1,0:T(8,128)(2,1)} %param.12) | copy-start | bytes 3145732
  407.3 2.0 copy-start.2
  407.3 3.3 copy-start.3
  421.4 1.3 copy-start.11
  476.8 9.6 %copy-start.1 = (bf16[3584,384]{1,0:T(8,128)(2,1)S(1)}, bf16[3584,384]{1,0:T(8,128)(2,1)}, u32[]{:S(2)}) copy-start(bf16[3584,384]{1,0:T(8,128)(2,1)} %param.13) | copy-start | bytes 8257540
Sparse Core Ops, SparseCore 0:
  9.6 83.4 all-gather.2
  94.6 148.0 all-gather.4
where the time goes:
time: 494 us; the launch traced here: 493 us
  waiting for transfers between devices  304 us (62%)
  Pallas kernels  91.2 us (18%)
  local copies, waits for them, and re-layouts  36.5 us (7%)
  matrix products  20.7 us (4%)
  starting transfers between devices  15 us (3%)
  between operations  14.3 us (3%)
  other arithmetic  11.5 us (2%)
    ppermute x23, waiting for transfers between devices, swap(): return lax.ppermute(value, 'ex', [(i, i ^ bit) for i in range(size)])  258 us
    all_gather x1, waiting for transfers between devices, body(): in_own = lax.all_gather(tokens, 'fsdp', axis=0, tiled=True)  45.6 us
    pallas_call x2, Pallas kernels, up_product(): pl.pallas_call(functools.partial(up_kernel, masks, width), out_shape=jax....  44.1 us
    pallas_call x1, Pallas kernels, down_product(): pl.pallas_call(functools.partial(down_kernel, masks, width), out_shape=[j...  30.3 us
    pallas_call x1, Pallas kernels, share(): pl.pallas_call(functools.partial(share_kernel, size, deep), out_shape=[ja...  16.8 us
    ppermute x23, starting transfers between devices, swap(): return lax.ppermute(value, 'ex', [(i, i ^ bit) for i in range(size)])  14.9 us
    unnamed x31, local copies, waits for them, and re-layouts  12.8 us
    dynamic_slice x3, local copies, waits for them, and re-layouts, halves(): theirs = lax.dynamic_slice_in_dim(weight, (1 - side) * half, half, axis)  9.94 us
  transfers between devices with their start and end apart: 25, of which 8 were waited for; matrix products, arithmetic and copies ran while one was open for 9% of the time, Pallas kernels for 9%

commit v1 on v0

--- a/solution.py
+++ b/solution.py
@@ -63,46 +63,80 @@
     )(place, rows, *[b for _, b in held])
 
 
-def down_kernel(masks, width, place_ref, y_ref, gate_ref, up_ref, proj_ref, *refs):
-    *blocks, b_ref, g_ref = refs
-    grad = None
+def down_dots(masks, width, dim, place_ref, y_ref, blocks):
+    sums = [None, None]
     for mask, block in zip(masks, blocks):
         start = pl.multiple_of((place_ref[0] ^ mask) * width, width)
-        piece = lax.dot_general(
-            y_ref[:, pl.ds(start, width)], block[...], (((1,), (1,)), ((), ())),
-            preferred_element_type=F32,
-        )
-        grad = piece if grad is None else grad + piece
-    gate = gate_ref[...]
-    up = up_ref[...]
-    sig = jax.nn.sigmoid(gate)
-    active = gate * sig
-    hidden = (active * up).astype(jnp.bfloat16)
-    d_gate = (grad * up * sig * (1.0 + gate * (1.0 - sig))).astype(jnp.bfloat16)
-    d_up = (grad * active).astype(jnp.bfloat16)
-    b = jnp.dot(hidden, proj_ref[:, :KB], preferred_element_type=F32)
-    g = jnp.dot(d_gate, proj_ref[:, KB : 2 * KB], preferred_element_type=F32)
-    g = g + jnp.dot(d_up, proj_ref[:, 2 * KB :], preferred_element_type=F32)
-
-    @pl.when(pl.program_id(0) == 0)
-    def _():
-        b_ref[...] = b
-        g_ref[...] = g
-
-    @pl.when(pl.program_id(0) > 0)
-    def _():
-        b_ref[...] += b
-        g_ref[...] += g
-
-
-def down_product(rows, gate, up, proj, held, place):
-    half = held[0][1].shape[0]
-    width = held[0][1].shape[1]
+        for k in range(2):
+            piece = lax.dot_general(
+                y_ref[:, pl.ds(start + k * dim, width)], block[...], (((1,), (1,)), ((), ())),
+                preferred_element_type=F32,
+            )
+            sums[k] = piece if sums[k] is None else sums[k] + piece
+    return sums
+
+
+def part_kernel(masks, width, dim, place_ref, y_ref, *refs):
+    *blocks, out_ref = refs
+    own, other = down_dots(masks, width, dim, place_ref, y_ref, blocks)
+    count = y_ref.shape[0]
+    out_ref[:count] = own
+    out_ref[count:] = other
+
+
+def part_product(rows, held, place):
+    half, width = held[0][1].shape
     tile = tile_of(half)
     masks = tuple(m for m, _ in held)
-    count = rows.shape[0]
+    count, dim = 2 * rows.shape[0], rows.shape[1] // 2
     return pl.pallas_call(
-        functools.partial(down_kernel, masks, width),
+        functools.partial(part_kernel, masks, width, dim),
+        out_shape=jax.ShapeDtypeStruct((count, half), F32),
+        grid_spec=pltpu.PrefetchScalarGridSpec(
+            num_scalar_prefetch=1,
+            grid=(half // tile,),
+            in_specs=[pl.BlockSpec(rows.shape, lambda t, p: (0, 0))]
+            + [pl.BlockSpec((tile, width), lambda t, p: (t, 0)) for _ in held],
+            out_specs=pl.BlockSpec((count, tile), lambda t, p: (0, t)),
+        ),
+        compiler_params=pltpu.CompilerParams(vmem_limit_bytes=VMEM_BYTES),
+    )(place, rows, *[b for _, b in held])
+
+
+def last_kernel(masks, width, dim, groups, place_ref, y_ref, part_ref, proj_ref, *refs):
+    gates, ups = refs[:groups], refs[groups : 2 * groups]
+    *blocks, b_ref, g_ref = refs[2 * groups :]
+    own, other = down_dots(masks, width, dim, place_ref, y_ref, blocks)
+    count = y_ref.shape[0]
+    first = pl.program_id(0) == 0
+    at = 0
+    for gate_ref, up_ref in zip(gates, ups):
+        gate = gate_ref[...]
+        up = up_ref[...]
+        rows = gate.shape[0]
+        fresh = own[at : at + rows] if at < count else other[at - count : at - count + rows]
+        grad = part_ref[at : at + rows] + fresh
+        sig = jax.nn.sigmoid(gate)
+        active = gate * sig
+        hidden = (active * up).astype(jnp.bfloat16)
+        d_gate = (grad * up * sig * (1.0 + gate * (1.0 - sig))).astype(jnp.bfloat16)
+        d_up = (grad * active).astype(jnp.bfloat16)
+        b = jnp.dot(hidden, proj_ref[:, :KB], preferred_element_type=F32)
+        g = jnp.dot(d_gate, proj_ref[:, KB : 2 * KB], preferred_element_type=F32)
+        g = g + jnp.dot(d_up, proj_ref[:, 2 * KB :], preferred_element_type=F32)
+        here = pl.ds(at, rows)
+        b_ref[here] = jnp.where(first, 0.0, b_ref[here]) + b
+        g_ref[here] = jnp.where(first, 0.0, g_ref[here]) + g
+        at += rows
+
+
+def last_product(rows, part, gates, ups, proj, held, place):
+    half, width = held[0][1].shape
+    tile = tile_of(half)
+    masks = tuple(m for m, _ in held)
+    count, dim = 2 * rows.shape[0], rows.shape[1] // 2
+    return pl.pallas_call(
+        functools.partial(last_kernel, masks, width, dim, len(gates)),
         out_shape=[jax.ShapeDtypeStruct((count, KB), F32)] * 2,
         grid_spec=pltpu.PrefetchScalarGridSpec(
             num_scalar_prefetch=1,
@@ -110,14 +144,14 @@
             in_specs=[
                 pl.BlockSpec(rows.shape, lambda t, p: (0, 0)),
                 pl.BlockSpec((count, tile), lambda t, p: (0, t)),
-                pl.BlockSpec((count, tile), lambda t, p: (0, t)),
                 pl.BlockSpec((tile, proj.shape[1]), lambda t, p: (t, 0)),
             ]
+            + [pl.BlockSpec((v.shape[0], tile), lambda t, p: (0, t)) for v in gates + ups]
             + [pl.BlockSpec((tile, width), lambda t, p: (t, 0)) for _ in held],
             out_specs=[pl.BlockSpec((count, KB), lambda t, p: (0, 0))] * 2,
         ),
         compiler_params=pltpu.CompilerParams(vmem_limit_bytes=VMEM_BYTES),
-    )(place, rows, gate, up, proj, *[b for _, b in held])
+    )(place, rows, part, proj, *gates, *ups, *[b for _, b in held])
 
 
 def share_kernel(
@@ -244,10 +278,8 @@
     )(part)
 
 
-def pair_product(left, right, count):
-    left_three = left.reshape(count, SEQ, left.shape[1])
-    right_three = right.reshape(count, SEQ, right.shape[1])
-    return jnp.einsum("esi,esj->eij", left_three, right_three, precision=lax.Precision.HIGHEST)
+def pair_product(left, right):
+    return jnp.einsum("esi,esj->eij", left, right, precision=lax.Precision.HIGHEST)
 
 
 def body(tokens, cotangent, gate_weight, up_weight, down_weight, model_proj, hidden_proj):
@@ -271,23 +303,42 @@
     cot_pair = jnp.concatenate([cotangent, swap(cotangent, top, size)], axis=1)
     cot_both = lax.all_gather(cot_pair, "fsdp", axis=0, tiled=True)
     dim = in_own.shape[1]
-    whole_in = jnp.concatenate([in_own, swap(in_own, top, size)], axis=0)
-    whole_cot = jnp.concatenate([cot_both[:, :dim], cot_both[:, dim:]], axis=0)
+    split = in_own.shape[0] // 2
+    ins = {
+        "own": in_own, "0": swap(in_own[:split], top, size), "1": swap(in_own[split:], top, size)
+    }
 
     gates = spread(gate_mine, swap(gate_theirs, top, size), top, size)
     ups = spread(up_mine, swap(up_theirs, top, size), top, size)
     downs = spread(down_mine, swap(down_theirs, top, size), top, size)
 
     where = place.astype(jnp.int32).reshape(1)
-    gate = up_product(whole_in, gates, where)
-    up = up_product(whole_in, ups, where)
-    proj_in = jnp.dot(whole_in, model_proj[:, :KA], preferred_element_type=F32)
-    proj_cot = jnp.dot(whole_cot, model_proj[:, KA:], preferred_element_type=F32)
+    late = top | (top // 2)
+    part = part_product(cot_both, [h for h in downs if h[0] & late != late], where)
+    gate, up, proj_in = [], [], []
+    proj_cot = [
+        jnp.dot(cot_both[:, k * dim : (k + 1) * dim], model_proj[:, KA:], preferred_element_type=F32)
+        for k in range(2)
+    ]
+    for name, rows in ins.items():
+        if name == "1":
+            rows, proj_in, proj_cot, up, part = lax.optimization_barrier(
+                (rows, proj_in, proj_cot, up, part)
+            )
+        gate.append(up_product(rows, gates, where))
+        up.append(up_product(rows, ups, where))
+        proj_in.append(jnp.dot(rows, model_proj[:, :KA], preferred_element_type=F32))
+    proj_in = [proj_in[0], jnp.concatenate(proj_in[1:], axis=0)]
     hp = lax.dynamic_slice_in_dim(hidden_proj, side * half, half, 0)
-    proj_hidden, proj_grad = down_product(whole_cot, gate, up, hp, downs, where)
-    part = pair_product(proj_in, proj_grad, 2) + pair_product(proj_cot, proj_hidden, 2)
+    proj_hidden, proj_grad = last_product(
+        cot_both, part, gate, up, hp, [h for h in downs if h[0] & late == late], where
+    )
+    part = pair_product(jnp.stack(proj_in), proj_grad.reshape(2, SEQ, KB)) + pair_product(
+        jnp.stack(proj_cot), proj_hidden.reshape(2, SEQ, KB)
+    )
     part = (part * (1.0 / math.sqrt(SEQ))).reshape(2, KA * KB)
-    part = jnp.where(side == 0, part, part[::-1])
+    own, other = part[:1], part[1:]
+    part = jnp.concatenate([jnp.where(side == 0, own, other), jnp.where(side == 0, other, own)])
     chunk = KA * KB // (2 * deep)
     part = part.reshape(2, 2 * deep, chunk).transpose(1, 0, 2)
     left, right = share(part, size, deep)

time: 494 us -> 449 us (0.909)
  waiting for transfers between devices: 304 us -> 245 us
  Pallas kernels: 91.2 us -> 128 us
  local copies, waits for them, and re-layouts: 36.5 us -> 13.3 us
  other arithmetic: 11.5 us -> 3.44 us
  matrix products: 20.7 us -> 26 us
    all_gather x1, waiting for transfers between devices: 45.6 us -> 0.02 us  [body(): in_own = lax.all_gather(tokens, 'fsdp', axis=0, tiled=True)]
    pallas_call x2 -> x6, Pallas kernels: 44.1 us -> 74.2 us  [up_product(): pl.pallas_call(functools.partial(up_kernel, masks, width), out_shape=jax....]
    ppermute x23 -> x24, waiting for transfers between devices: 258 us -> 244 us  [swap(): return lax.ppermute(value, 'ex', [(i, i ^ bit) for i in range(size)])]
    unnamed x31 -> x29, local copies, waits for them, and re-layouts: 12.8 us -> 0.82 us
    concatenate x1 -> x0, other arithmetic: 7.98 us -> none  [body(): whole_cot = jnp.concatenate([cot_both[:, :dim], cot_both[:, dim:]], axis=0)]
    pallas_call x1 -> x2, Pallas kernels: 30.3 us -> 36.6 us  [the longest x1 18.5 us: last_product(): pl.pallas_call(functools.partial(last_kernel, masks, width, dim, len(gate...]
    dynamic_slice x3, local copies, waits for them, and re-layouts: 9.94 us -> 4.21 us  [halves(): theirs = lax.dynamic_slice_in_dim(weight, (1 - side) * half, half, axis)]
    dot_general x4 -> x7, matrix products: 11.7 us -> 17 us  [the longest x3 8.28 us: body(): jnp.dot(rows, model_proj[:, :KA], preferred_element_type=F32)]
  transfers between devices with their start and end apart: 25 -> 26, of which waited for: 8 -> 10; matrix products, arithmetic and copies ran while one was open for 9% -> 6% of each run, Pallas kernels for 9% -> 21%
where the time goes in v1:
time: 449 us; the launch traced here: 448 us
  waiting for transfers between devices  245 us (55%)
  Pallas kernels  128 us (29%)
  matrix products  26 us (6%)
  starting transfers between devices  17.1 us (4%)
  between operations  14.3 us (3%)
  local copies, waits for them, and re-layouts  13.3 us (3%)
    ppermute x24, waiting for transfers between devices, swap(): return lax.ppermute(value, 'ex', [(i, i ^ bit) for i in range(size)])  244 us
    pallas_call x6, Pallas kernels, up_product(): pl.pallas_call(functools.partial(up_kernel, masks, width), out_shape=jax....  74.2 us
    pallas_call x1, Pallas kernels, last_product(): pl.pallas_call(functools.partial(last_kernel, masks, width, dim, len(gate...  18.5 us
    pallas_call x1, Pallas kernels, part_product(): pl.pallas_call(functools.partial(part_kernel, masks, width, dim), out_sha...  18.1 us
    pallas_call x1, Pallas kernels, share(): pl.pallas_call(functools.partial(share_kernel, size, deep), out_shape=[ja...  17.6 us
    ppermute x24, starting transfers between devices, swap(): return lax.ppermute(value, 'ex', [(i, i ^ bit) for i in range(size)])  17.1 us
    dot_general x1, matrix products, body(): gram = jnp.dot(left.T, right, precision=lax.Precision.HIGHEST) / size  8.99 us
  transfers between devices with their start and end apart: 26, of which 10 were waited for; matrix products, arithmetic and copies ran while one was open for 6% of the time, Pallas kernels for 21%

profile of v1, /device:TPU:0, one launch (start us, length us, event | category | flops | bytes accessed | tf_op | source)
XLA Modules:
  0.0 447.7 jit_solution(11160953192053182754)
XLA Ops:
  7.2 0.0 copy-start
  7.2 0.0 all-gather.3.cloned.1.call-start
  7.2 0.7 all-gather.3.cloned.1.call-update
  7.9 0.0 all-gather.5.cloned.1.call-start
  8.0 3.1 collective-permute-start.2
  11.0 23.4 %collective-permute-done.2 = bf16[128,4096]{1,0:T(8,128)(2,1)S(1)} collective-permute-done((bf16[128,4096]{1,0:T(8,128)(2,1)}, bf16[128,4096]{1,0:T(8,128)(2,1)S(1)}, u32[]{:S(2)}, u32[]{:S(2)}) %collective-permute-start.2) | collective-permute-done | bytes 1048608 | tf_op jit(solution)/shard_map/ppermute | solution.py:20
  34.4 2.7 pad_maximum_fusion
  37.1 0.0 all-gather.5.cloned.1.call-update
  37.2 3.7 constant_dynamic-slice_fusion.4
  40.9 1.7 collective-permute-start.10
  42.7 1.5 collective-permute-start.11
  44.2 0.2 constant_dynamic-slice_fusion.6
  44.4 0.6 collective-permute-start.3
  45.0 0.3 collective-permute-start.4
  45.3 0.2 constant_dynamic-slice_fusion.1
  45.5 0.2 copy-done.3
  45.7 38.2 %collective-permute-done.10.refs_1_ = bf16[1792,512]{1,0:T(8,128)(2,1)} collective-permute-done((bf16[1792,512]{1,0:T(8,128)(2,1)S(1)}, bf16[1792,512]{1,0:T(8,128)(2,1)}, u32[]{:S(2)}, u32[]{:S(2)}) %collective-permute-start.10) | collective-permute-done | bytes 1835040 | tf_op jit(solution)/shard_map/ppermute | solution.py:20
  83.9 1.7 collective-permute-start.15
  85.7 0.2 collective-permute-done.11.refs_2_
  85.9 1.5 collective-permute-start.16
  87.4 35.8 %collective-permute-done.3.refs_1_ = bf16[512,1792]{1,0:T(8,128)(2,1)S(1)} collective-permute-done((bf16[512,1792]{1,0:T(8,128)(2,1)S(1)}, bf16[512,1792]{1,0:T(8,128)(2,1)S(1)}, u32[]{:S(2)}, u32[]{:S(2)}) %collective-permute-start.3) | collective-permute-done | bytes 1835040 | tf_op jit(solution)/shard_map/ppermute | solution.py:20
  123.1 2.0 collective-permute-done.4.refs_2_
  125.1 1.5 collective-permute-start.5
  126.6 0.1 collective-permute-start.7
  126.7 34.3 %collective-permute-done.15.refs_1_ = bf16[512,1792]{1,0:T(8,128)(2,1)} collective-permute-done((bf16[512,1792]{1,0:T(8,128)(2,1)S(1)}, bf16[512,1792]{1,0:T(8,128)(2,1)}, u32[]{:S(2)}, u32[]{:S(2)}) %collective-permute-start.15) | collective-permute-done | bytes 1835040 | tf_op jit(solution)/shard_map/ppermute | solution.py:20
  161.0 3.6 collective-permute-done.16.refs_2_
  164.5 1.5 collective-permute-start.17
  166.0 0.1 collective-permute-start.19
  166.1 37.7 %collective-permute-done.5.refs_3_ = bf16[512,1792]{1,0:T(8,128)(2,1)} collective-permute-done((bf16[512,1792]{1,0:T(8,128)(2,1)S(1)}, bf16[512,1792]{1,0:T(8,128)(2,1)}, u32[]{:S(2)}, u32[]{:S(2)}) %collective-permute-start.5) | collective-permute-done | bytes 1835040 | tf_op jit(solution)/shard_map/ppermute | solution.py:20
  203.9 1.6 collective-permute-start.22
  205.4 0.3 collective-permute-start.9
  205.7 37.5 %collective-permute-done.17.refs_3_ = bf16[512,1792]{1,0:T(8,128)(2,1)} collective-permute-done((bf16[512,1792]{1,0:T(8,128)(2,1)}, bf16[512,1792]{1,0:T(8,128)(2,1)}, u32[]{:S(2)}, u32[]{:S(2)}) %collective-permute-start.17) | collective-permute-done | bytes 1835040 | tf_op jit(solution)/shard_map/ppermute | solution.py:20
  243.2 0.0 all-gather.3.cloned.1.call-done.x_ref
  243.2 4.7 %fusion.22 = (bf16[256,4096]{1,0:T(8,128)(2,1)}, bf16[256,4096]{1,0:T(8,128)(2,1)}) fusion(bf16[512,4096]{1,0:T(8,128)(2,1)} %all-gather.3.cloned.1.call-done.x_ref), kind=kLoop, calls=%fused_computation.37 | loop fusion | bytes 8388608 | tf_op jit(solution)/shard_map/slice | solution.py:308
  247.9 0.3 collective-permute-start.1
  248.2 0.3 collective-permute-start.12
  248.5 31.8 %collective-permute-done.22.refs_6_ = bf16[1792,512]{1,0:T(8,128)(2,1)} collective-permute-done((bf16[1792,512]{1,0:T(8,128)(2,1)}, bf16[1792,512]{1,0:T(8,128)(2,1)}, u32[]{:S(2)}, u32[]{:S(2)}) %collective-permute-start.22) | collective-permute-done | bytes 1835040 | tf_op jit(solution)/shard_map/ppermute | solution.py:20
  280.3 0.5 collective-permute-start.14
  280.8 0.6 collective-permute-start
  281.4 1.2 constant_dynamic-slice_fusion.3.proj_ref
  282.6 14.4 %shard_map.86.refs_3_ = f32[512,1792]{1,0:T(8,128)} custom-call(s32[1]{0:T(128)} %bitcast.place_ref, bf16[512,4096]{1,0:T(8,128)(2,1)} %all-gather.3.cloned.1.call-done.x_ref, bf16[512,1792]{1,0:T(8,128)(2,1)} %copy-done.3, bf16[512,1792]{1,0:T(8,128)(2,1)} %copy-done.5, bf16[512,1792]{1,0:T(8,128)(2,1)} %copy-done.6, ...), custom_call_target="tpu_custom_call" | custom-call | tf_op jit(solution)/shard_map/pallas_call | solution.py:52
  297.1 14.5 %shard_map.89.refs_0_ = f32[512,1792]{1,0:T(8,128)} custom-call(s32[1]{0:T(128)} %bitcast.place_ref, bf16[512,4096]{1,0:T(8,128)(2,1)} %all-gather.3.cloned.1.call-done.x_ref, bf16[512,1792]{1,0:T(8,128)(2,1)} %copy-done.4, bf16[512,1792]{1,0:T(8,128)(2,1)} %collective-permute-done.15.refs_1_, bf16[512,1792]{1,0:T(8,128)(2,1)} %collective-permute-done.16.refs_2_, ...), custom_call_target="tpu_custom_call" | custom-call | tf_op jit(solution)/shard_map/pallas_call | solution.py:52
  311.5 0.1 collective-permute-start.23
  311.6 3.6 fusion.11
  315.2 11.4 %shard_map.87.refs_4_ = f32[256,1792]{1,0:T(8,128)} custom-call(s32[1]{0:T(128)} %bitcast.place_ref, bf16[256,4096]{1,0:T(8,128)(2,1)} %collective-permute-done.1.x_ref, bf16[512,1792]{1,0:T(8,128)(2,1)} %copy-done.3, bf16[512,1792]{1,0:T(8,128)(2,1)} %copy-done.5, bf16[512,1792]{1,0:T(8,128)(2,1)} %copy-done.6, ...), custom_call_target="tpu_custom_call" | custom-call | tf_op jit(solution)/shard_map/pallas_call | solution.py:52
  326.6 11.3 %shard_map.90.refs_1_ = f32[256,1792]{1,0:T(8,128)} custom-call(s32[1]{0:T(128)} %bitcast.place_ref, bf16[256,4096]{1,0:T(8,128)(2,1)} %collective-permute-done.1.x_ref, bf16[512,1792]{1,0:T(8,128)(2,1)} %copy-done.4, bf16[512,1792]{1,0:T(8,128)(2,1)} %collective-permute-done.15.refs_1_, bf16[512,1792]{1,0:T(8,128)(2,1)} %collective-permute-done.16.refs_2_, ...), custom_call_target="tpu_custom_call" | custom-call | tf_op jit(solution)/shard_map/pallas_call | solution.py:52
  337.9 2.3 fusion.9
  340.3 0.0 all-gather.5.cloned.1.call-done.y_ref
  340.3 18.1 %shard_map.88.part_ref = f32[1024,1792]{1,0:T(8,128)} custom-call(s32[1]{0:T(128)} %bitcast.place_ref, bf16[512,8192]{1,0:T(8,128)(2,1)} %all-gather.5.cloned.1.call-done.y_ref, bf16[1792,512]{1,0:T(8,128)(2,1)} %get-tuple-element.31.refs_0_, bf16[1792,512]{1,0:T(8,128)(2,1)} %collective-permute-done.10.refs_1_, ...), custom_call_target="tpu_custom_call" | custom-call | tf_op jit(solution)/shard_map/pallas_call | solution.py:92
  358.4 4.1 fusion
  362.4 0.6 copy-done.2
  363.0 1.7 fusion.2
  364.8 11.4 %shard_map.92.refs_5_ = f32[256,1792]{1,0:T(8,128)} custom-call(s32[1]{0:T(128)} %bitcast.place_ref, bf16[256,4096]{1,0:T(8,128)(2,1)} %collective-permute-done.x_ref, bf16[512,1792]{1,0:T(8,128)(2,1)} %copy-done.3, bf16[512,1792]{1,0:T(8,128)(2,1)} %copy-done.5, bf16[512,1792]{1,0:T(8,128)(2,1)} %copy-done.6, ...), custom_call_target="tpu_custom_call" | custom-call | tf_op jit(solution)/shard_map/pallas_call | solution.py:52
  376.1 11.3 %shard_map.91.refs_2_ = f32[256,1792]{1,0:T(8,128)} custom-call(s32[1]{0:T(128)} %bitcast.place_ref, bf16[256,4096]{1,0:T(8,128)(2,1)} %collective-permute-done.x_ref, bf16[512,1792]{1,0:T(8,128)(2,1)} %copy-done.4, bf16[512,1792]{1,0:T(8,128)(2,1)} %collective-permute-done.15.refs_1_, bf16[512,1792]{1,0:T(8,128)(2,1)} %collective-permute-done.16.refs_2_, ...), custom_call_target="tpu_custom_call" | custom-call | tf_op jit(solution)/shard_map/pallas_call | solution.py:52
  387.4 2.3 fusion.7
  389.8 18.5 %shard_map.93 = (f32[1024,128]{1,0:T(8,128)}, f32[1024,128]{1,0:T(8,128)}) custom-call(s32[1]{0:T(128)} %bitcast.place_ref, bf16[512,8192]{1,0:T(8,128)(2,1)} %all-gather.5.cloned.1.call-done.y_ref, f32[1024,1792]{1,0:T(8,128)} %shard_map.88.part_ref, bf16[1792,384]{1,0:T(8,128)(2,1)} %constant_dynamic-slice_fusion.3.proj_ref, ...), custom_call_target="tpu_custom_call" | custom-call | tf_op jit(solution)/shard_map/pallas_call | solution.py:138
  408.3 1.5 fusion.16
  409.8 1.5 fusion.4
  411.3 0.7 maximum_bitcast_fusion.1.part_ref
  412.0 17.6 %shard_map.94 = (f32[4,2,2,1024]{3,2,1,0:T(2,128)}, f32[4,1,2,1024]{3,2,1,0:T(2,128)}) custom-call(f32[8,2,1024]{2,1,0:T(2,128)} %maximum_bitcast_fusion.1.part_ref), custom_call_target="tpu_custom_call" | custom-call | tf_op jit(solution)/shard_map/pallas_call | solution.py:263
  429.5 0.9 copy.9
  430.4 0.8 copy.10
  431.2 9.0 %convolution_multiply_fusion = f32[2048,1024]{1,0:T(8,128)} fusion(f32[8,2048]{1,0:T(8,128)S(1)} %bitcast.27, f32[8,1024]{1,0:T(8,128)S(1)} %reshape.77), kind=kOutput, calls=%fused_computation | convolution fusion | flops 203423744 | bytes 8486912 | tf_op jit(solution)/shard_map/dot_general | solution.py:348
  440.2 0.6 constant_dynamic-slice_fusion
  (49 shorter events, 0.2 us)
Async XLA Ops:
  7.2 274.2 %copy-start = (bf16[3584,384]{1,0:T(8,128)(2,1)S(1)}, bf16[3584,384]{1,0:T(8,128)(2,1)}, u32[]{:S(2)}) copy-start(bf16[3584,384]{1,0:T(8,128)(2,1)} %param.13) | copy-start | bytes 8257540
  7.2 236.0 %all-gather.3.cloned.1.call-start = ((), (), s32[]{:S(2)}) async-start(), calls=%async_computation | async-start | bytes 5242880 | tf_op jit(solution)/shard_map/all_gather | solution.py:302
  7.9 332.4 %all-gather.5.cloned.1.call-start = ((), (), s32[]{:S(2)}) async-start(), calls=%async_computation.1 | async-start | bytes 10485760 | tf_op jit(solution)/shard_map/all_gather | solution.py:304
  8.0 26.4 %collective-permute-start.2 = (bf16[128,4096]{1,0:T(8,128)(2,1)}, bf16[128,4096]{1,0:T(8,128)(2,1)S(1)}, u32[]{:S(2)}, u32[]{:S(2)}) collective-permute-start(bf16[128,4096]{1,0:T(8,128)(2,1)} %param.8), channel_id=1, source_target_pairs={{0,16},{4,20},{8,24},{12,28},{16,0},{20,4},{24,8},{28,12},{1,17},{... | collective-permute-start | bytes 3145736 | tf_op jit(solution)/shard_map/ppermute | solution.py:20
  37.2 7.0 %copy-start.12 = (bf16[512,3584]{1,0:T(8,128)(2,1)S(1)}, bf16[512,3584]{1,0:T(8,128)(2,1)}, u32[]{:S(2)}) copy-start(bf16[512,3584]{1,0:T(8,128)(2,1)} %param.10) | copy-start | bytes 11010052
  40.9 43.0 %collective-permute-start.10 = (bf16[1792,512]{1,0:T(8,128)(2,1)S(1)}, bf16[1792,512]{1,0:T(8,128)(2,1)}, u32[]{:S(2)}, u32[]{:S(2)}) collective-permute-start(bf16[1792,512]{1,0:T(8,128)(2,1)S(1)} %get-tuple-element.30), channel_id=1, source_target_pairs={{0,16},{4,20},{8,24},{12,28},{16,0},{20,4},{24,8},{28,12},{1,17},{... | collective-permute-start | bytes 5505032 | tf_op jit(solution)/shard_map/ppermute | solution.py:20
  42.7 2.6 copy-start.13
  42.7 43.2 %collective-permute-start.11 = (bf16[1792,512]{1,0:T(8,128)(2,1)}, bf16[1792,512]{1,0:T(8,128)(2,1)}, u32[]{:S(2)}, u32[]{:S(2)}) collective-permute-start(bf16[1792,512]{1,0:T(8,128)(2,1)} %get-tuple-element.31.refs_0_), channel_id=1, source_target_pairs={{0,8},{4,12},{8,0},{12,4},{16,24},{20,28},{24,16},{28,20},{1,9},{5... | collective-permute-start | bytes 5505032 | tf_op jit(solution)/shard_map/ppermute | solution.py:20
  44.4 1.3 copy-start.3
  44.4 78.7 %collective-permute-start.3 = (bf16[512,1792]{1,0:T(8,128)(2,1)S(1)}, bf16[512,1792]{1,0:T(8,128)(2,1)S(1)}, u32[]{:S(2)}, u32[]{:S(2)}) collective-permute-start(bf16[512,1792]{1,0:T(8,128)(2,1)S(1)} %get-tuple-element.32), channel_id=1, source_target_pairs={{0,16},{4,20},{8,24},{12,28},{16,0},{20,4},{24,8},{28,12},{1,17},{... | collective-permute-start | bytes 5505032 | tf_op jit(solution)/shard_map/ppermute | solution.py:20
  45.0 80.1 %collective-permute-start.4 = (bf16[512,1792]{1,0:T(8,128)(2,1)S(1)}, bf16[512,1792]{1,0:T(8,128)(2,1)S(1)}, u32[]{:S(2)}, u32[]{:S(2)}) collective-permute-start(bf16[512,1792]{1,0:T(8,128)(2,1)S(1)} %get-tuple-element.33.refs_0_), channel_id=1, source_target_pairs={{0,8},{4,12},{8,0},{12,4},{16,24},{20,28},{24,16},{28,20},{1,9},{5... | collective-permute-start | bytes 5505032 | tf_op jit(solution)/shard_map/ppermute | solution.py:20
  45.3 81.3 %collective-permute-start.6 = (bf16[512,1792]{1,0:T(8,128)(2,1)S(1)}, bf16[512,1792]{1,0:T(8,128)(2,1)S(1)}, u32[]{:S(2)}, u32[]{:S(2)}) collective-permute-start(bf16[512,1792]{1,0:T(8,128)(2,1)S(1)} %get-tuple-element.33.refs_0_), channel_id=1, source_target_pairs={{0,4},{4,0},{8,12},{12,8},{16,20},{20,16},{24,28},{28,24},{1,5},{5... | collective-permute-start | bytes 5505032 | tf_op jit(solution)/shard_map/ppermute | solution.py:20
  45.7 80.9 %copy-start.4 = (bf16[512,1792]{1,0:T(8,128)(2,1)}, bf16[512,1792]{1,0:T(8,128)(2,1)S(1)}, u32[]{:S(2)}) copy-start(bf16[512,1792]{1,0:T(8,128)(2,1)S(1)} %get-tuple-element.29.refs_0_) | copy-start | bytes 5505028
  83.9 77.0 %collective-permute-start.15 = (bf16[512,1792]{1,0:T(8,128)(2,1)S(1)}, bf16[512,1792]{1,0:T(8,128)(2,1)}, u32[]{:S(2)}, u32[]{:S(2)}) collective-permute-start(bf16[512,1792]{1,0:T(8,128)(2,1)S(1)} %get-tuple-element.28), channel_id=1, source_target_pairs={{0,16},{4,20},{8,24},{12,28},{16,0},{20,4},{24,8},{28,12},{1,17},{... | collective-permute-start | bytes 5505032 | tf_op jit(solution)/shard_map/ppermute | solution.py:20
  85.9 78.6 %collective-permute-start.16 = (bf16[512,1792]{1,0:T(8,128)(2,1)S(1)}, bf16[512,1792]{1,0:T(8,128)(2,1)}, u32[]{:S(2)}, u32[]{:S(2)}) collective-permute-start(bf16[512,1792]{1,0:T(8,128)(2,1)S(1)} %get-tuple-element.29.refs_0_), channel_id=1, source_target_pairs={{0,8},{4,12},{8,0},{12,4},{16,24},{20,28},{24,16},{28,20},{1,9},{5... | collective-permute-start | bytes 5505032 | tf_op jit(solution)/shard_map/ppermute | solution.py:20
  123.1 42.9 %copy-start.5 = (bf16[512,1792]{1,0:T(8,128)(2,1)}, bf16[512,1792]{1,0:T(8,128)(2,1)S(1)}, u32[]{:S(2)}) copy-start(bf16[512,1792]{1,0:T(8,128)(2,1)S(1)} %collective-permute-done.3.refs_1_) | copy-start | bytes 5505028
  123.1 42.9 %collective-permute-start.18 = (bf16[512,1792]{1,0:T(8,128)(2,1)S(1)}, bf16[512,1792]{1,0:T(8,128)(2,1)S(1)}, u32[]{:S(2)}, u32[]{:S(2)}) collective-permute-start(bf16[512,1792]{1,0:T(8,128)(2,1)S(1)} %get-tuple-element.29.refs_0_), channel_id=1, source_target_pairs={{0,4},{4,0},{8,12},{12,8},{16,20},{20,16},{24,28},{28,24},{1,5},{5... | collective-permute-start | bytes 5505032 | tf_op jit(solution)/shard_map/ppermute | solution.py:20
  125.1 78.8 %copy-start.6 = (bf16[512,1792]{1,0:T(8,128)(2,1)}, bf16[512,1792]{1,0:T(8,128)(2,1)S(1)}, u32[]{:S(2)}) copy-start(bf16[512,1792]{1,0:T(8,128)(2,1)S(1)} %collective-permute-done.4.refs_2_) | copy-start | bytes 5505028
  125.1 78.8 %collective-permute-start.5 = (bf16[512,1792]{1,0:T(8,128)(2,1)S(1)}, bf16[512,1792]{1,0:T(8,128)(2,1)}, u32[]{:S(2)}, u32[]{:S(2)}) collective-permute-start(bf16[512,1792]{1,0:T(8,128)(2,1)S(1)} %collective-permute-done.3.refs_1_), channel_id=1, source_target_pairs={{0,8},{4,12},{8,0},{12,4},{16,24},{20,28},{24,16},{28,20},{1,9},{5... | collective-permute-start | bytes 5505032 | tf_op jit(solution)/shard_map/ppermute | solution.py:20
  126.6 78.8 %copy-start.7 = (bf16[512,1792]{1,0:T(8,128)(2,1)}, bf16[512,1792]{1,0:T(8,128)(2,1)S(1)}, u32[]{:S(2)}) copy-start(bf16[512,1792]{1,0:T(8,128)(2,1)S(1)} %collective-permute-done.6.refs_4_) | copy-start | bytes 5505028
  126.6 77.3 %collective-permute-start.7 = (bf16[512,1792]{1,0:T(8,128)(2,1)S(1)}, bf16[512,1792]{1,0:T(8,128)(2,1)S(1)}, u32[]{:S(2)}, u32[]{:S(2)}) collective-permute-start(bf16[512,1792]{1,0:T(8,128)(2,1)S(1)} %collective-permute-done.3.refs_1_), channel_id=1, source_target_pairs={{0,4},{4,0},{8,12},{12,8},{16,20},{20,16},{24,28},{28,24},{1,5},{5... | collective-permute-start | bytes 5505032 | tf_op jit(solution)/shard_map/ppermute | solution.py:20
  161.0 44.5 %collective-permute-start.8 = (bf16[512,1792]{1,0:T(8,128)(2,1)S(1)}, bf16[512,1792]{1,0:T(8,128)(2,1)S(1)}, u32[]{:S(2)}, u32[]{:S(2)}) collective-permute-start(bf16[512,1792]{1,0:T(8,128)(2,1)S(1)} %collective-permute-done.4.refs_2_), channel_id=1, source_target_pairs={{0,4},{4,0},{8,12},{12,8},{16,20},{20,16},{24,28},{28,24},{1,5},{5... | collective-permute-start | bytes 5505032 | tf_op jit(solution)/shard_map/ppermute | solution.py:20
  164.5 78.6 %collective-permute-start.17 = (bf16[512,1792]{1,0:T(8,128)(2,1)}, bf16[512,1792]{1,0:T(8,128)(2,1)}, u32[]{:S(2)}, u32[]{:S(2)}) collective-permute-start(bf16[512,1792]{1,0:T(8,128)(2,1)} %collective-permute-done.15.refs_1_), channel_id=1, source_target_pairs={{0,8},{4,12},{8,0},{12,4},{16,24},{20,28},{24,16},{28,20},{1,9},{5... | collective-permute-start | bytes 5505032 | tf_op jit(solution)/shard_map/ppermute | solution.py:20
  166.0 39.7 %copy-start.8 = (bf16[512,1792]{1,0:T(8,128)(2,1)}, bf16[512,1792]{1,0:T(8,128)(2,1)S(1)}, u32[]{:S(2)}) copy-start(bf16[512,1792]{1,0:T(8,128)(2,1)S(1)} %collective-permute-done.18.refs_4_) | copy-start | bytes 5505028
  166.0 81.9 %collective-permute-start.19 = (bf16[512,1792]{1,0:T(8,128)(2,1)}, bf16[512,1792]{1,0:T(8,128)(2,1)}, u32[]{:S(2)}, u32[]{:S(2)}) collective-permute-start(bf16[512,1792]{1,0:T(8,128)(2,1)} %collective-permute-done.15.refs_1_), channel_id=1, source_target_pairs={{0,4},{4,0},{8,12},{12,8},{16,20},{20,16},{24,28},{28,24},{1,5},{5... | collective-permute-start | bytes 5505032 | tf_op jit(solution)/shard_map/ppermute | solution.py:20
  203.8 44.4 %collective-permute-start.20 = (bf16[512,1792]{1,0:T(8,128)(2,1)}, bf16[512,1792]{1,0:T(8,128)(2,1)}, u32[]{:S(2)}, u32[]{:S(2)}) collective-permute-start(bf16[512,1792]{1,0:T(8,128)(2,1)} %collective-permute-done.16.refs_2_), channel_id=1, source_target_pairs={{0,4},{4,0},{8,12},{12,8},{16,20},{20,16},{24,28},{28,24},{1,5},{5... | collective-permute-start | bytes 5505032 | tf_op jit(solution)/shard_map/ppermute | solution.py:20
  203.9 39.3 %copy-start.9 = (bf16[512,1792]{1,0:T(8,128)(2,1)}, bf16[512,1792]{1,0:T(8,128)(2,1)S(1)}, u32[]{:S(2)}) copy-start(bf16[512,1792]{1,0:T(8,128)(2,1)S(1)} %collective-permute-done.7.refs_5_) | copy-start | bytes 5505028
  203.9 76.5 %collective-permute-start.22 = (bf16[1792,512]{1,0:T(8,128)(2,1)}, bf16[1792,512]{1,0:T(8,128)(2,1)}, u32[]{:S(2)}, u32[]{:S(2)}) collective-permute-start(bf16[1792,512]{1,0:T(8,128)(2,1)} %collective-permute-done.10.refs_1_), channel_id=1, source_target_pairs={{0,8},{4,12},{8,0},{12,4},{16,24},{20,28},{24,16},{28,20},{1,9},{5... | collective-permute-start | bytes 5505032 | tf_op jit(solution)/shard_map/ppermute | solution.py:20
  205.4 37.7 %copy-start.10 = (bf16[512,1792]{1,0:T(8,128)(2,1)}, bf16[512,1792]{1,0:T(8,128)(2,1)S(1)}, u32[]{:S(2)}) copy-start(bf16[512,1792]{1,0:T(8,128)(2,1)S(1)} %collective-permute-done.8.refs_6_) | copy-start | bytes 5505028
  205.4 74.9 %collective-permute-start.9 = (bf16[512,1792]{1,0:T(8,128)(2,1)}, bf16[512,1792]{1,0:T(8,128)(2,1)}, u32[]{:S(2)}, u32[]{:S(2)}) collective-permute-start(bf16[512,1792]{1,0:T(8,128)(2,1)} %collective-permute-done.5.refs_3_), channel_id=1, source_target_pairs={{0,4},{4,0},{8,12},{12,8},{16,20},{20,16},{24,28},{28,24},{1,5},{5... | collective-permute-start | bytes 5505032 | tf_op jit(solution)/shard_map/ppermute | solution.py:20
  243.2 37.7 %collective-permute-start.21 = (bf16[512,1792]{1,0:T(8,128)(2,1)}, bf16[512,1792]{1,0:T(8,128)(2,1)}, u32[]{:S(2)}, u32[]{:S(2)}) collective-permute-start(bf16[512,1792]{1,0:T(8,128)(2,1)} %collective-permute-done.17.refs_3_), channel_id=1, source_target_pairs={{0,4},{4,0},{8,12},{12,8},{16,20},{20,16},{24,28},{28,24},{1,5},{5... | collective-permute-start | bytes 5505032 | tf_op jit(solution)/shard_map/ppermute | solution.py:20
  247.9 63.6 %collective-permute-start.1 = (bf16[256,4096]{1,0:T(8,128)(2,1)}, bf16[256,4096]{1,0:T(8,128)(2,1)}, u32[]{:S(2)}, u32[]{:S(2)}) collective-permute-start(bf16[256,4096]{1,0:T(8,128)(2,1)} %get-tuple-element.26), channel_id=1, source_target_pairs={{0,16},{4,20},{8,24},{12,28},{16,0},{20,4},{24,8},{28,12},{1,17},{... | collective-permute-start | bytes 6291464 | tf_op jit(solution)/shard_map/ppermute | solution.py:20
  248.2 92.0 %collective-permute-start.12 = (bf16[1792,512]{1,0:T(8,128)(2,1)}, bf16[1792,512]{1,0:T(8,128)(2,1)}, u32[]{:S(2)}, u32[]{:S(2)}) collective-permute-start(bf16[1792,512]{1,0:T(8,128)(2,1)} %get-tuple-element.31.refs_0_), channel_id=1, source_target_pairs={{0,4},{4,0},{8,12},{12,8},{16,20},{20,16},{24,28},{28,24},{1,5},{5... | collective-permute-start | bytes 5505032 | tf_op jit(solution)/shard_map/ppermute | solution.py:20
  280.3 59.9 %collective-permute-start.13 = (bf16[1792,512]{1,0:T(8,128)(2,1)}, bf16[1792,512]{1,0:T(8,128)(2,1)}, u32[]{:S(2)}, u32[]{:S(2)}) collective-permute-start(bf16[1792,512]{1,0:T(8,128)(2,1)} %collective-permute-done.10.refs_1_), channel_id=1, source_target_pairs={{0,4},{4,0},{8,12},{12,8},{16,20},{20,16},{24,28},{28,24},{1,5},{5... | collective-permute-start | bytes 5505032 | tf_op jit(solution)/shard_map/ppermute | solution.py:20
  280.3 59.9 %collective-permute-start.14 = (bf16[1792,512]{1,0:T(8,128)(2,1)}, bf16[1792,512]{1,0:T(8,128)(2,1)}, u32[]{:S(2)}, u32[]{:S(2)}) collective-permute-start(bf16[1792,512]{1,0:T(8,128)(2,1)} %collective-permute-done.11.refs_2_), channel_id=1, source_target_pairs={{0,4},{4,0},{8,12},{12,8},{16,20},{20,16},{24,28},{28,24},{1,5},{5... | collective-permute-start | bytes 5505032 | tf_op jit(solution)/shard_map/ppermute | solution.py:20
  280.8 83.9 %collective-permute-start = (bf16[256,4096]{1,0:T(8,128)(2,1)}, bf16[256,4096]{1,0:T(8,128)(2,1)}, u32[]{:S(2)}, u32[]{:S(2)}) collective-permute-start(bf16[256,4096]{1,0:T(8,128)(2,1)} %get-tuple-element.27), channel_id=1, source_target_pairs={{0,16},{4,20},{8,24},{12,28},{16,0},{20,4},{24,8},{28,12},{1,17},{... | collective-permute-start | bytes 6291464 | tf_op jit(solution)/shard_map/ppermute | solution.py:20
  297.1 14.6 %copy-start.11 = (bf16[4096,128]{1,0:T(8,128)(2,1)S(1)}, bf16[4096,128]{1,0:T(8,128)(2,1)}, u32[]{:S(2)}) copy-start(bf16[4096,128]{1,0:T(8,128)(2,1)} %param.12) | copy-start | bytes 3145732
  311.5 78.3 %collective-permute-start.23 = (bf16[1792,512]{1,0:T(8,128)(2,1)}, bf16[1792,512]{1,0:T(8,128)(2,1)}, u32[]{:S(2)}, u32[]{:S(2)}) collective-permute-start(bf16[1792,512]{1,0:T(8,128)(2,1)} %collective-permute-done.22.refs_6_), channel_id=1, source_target_pairs={{0,4},{4,0},{8,12},{12,8},{16,20},{20,16},{24,28},{28,24},{1,5},{5... | collective-permute-start | bytes 5505032 | tf_op jit(solution)/shard_map/ppermute | solution.py:20
  358.4 4.6 %copy-start.2 = (bf16[512,8192]{1,0:T(8,128)(2,1)S(1)}, bf16[512,8192]{1,0:T(8,128)(2,1)}, u32[]{:S(2)}) copy-start(bf16[512,8192]{1,0:T(8,128)(2,1)} %all-gather.5.cloned.1.call-done.y_ref) | copy-start | bytes 25165828
  431.2 9.6 %copy-start.1 = (bf16[3584,384]{1,0:T(8,128)(2,1)S(1)}, bf16[3584,384]{1,0:T(8,128)(2,1)}, u32[]{:S(2)}) copy-start(bf16[3584,384]{1,0:T(8,128)(2,1)} %param.13) | copy-start | bytes 8257540
Sparse Core Ops, SparseCore 0:
  9.6 83.4 all-gather.2
  95.2 148.0 all-gather.4

commit v2 on v1

--- a/solution.py
+++ b/solution.py
@@ -280,6 +280,38 @@
 
 def pair_product(left, right):
     return jnp.einsum("esi,esj->eij", left, right, precision=lax.Precision.HIGHEST)
+
+
+def pieces(value):
+    high = value.astype(jnp.bfloat16)
+    rest = value - high.astype(F32)
+    mid = rest.astype(jnp.bfloat16)
+    low = (rest - mid.astype(F32)).astype(jnp.bfloat16)
+    return high, mid, low
+
+
+def gram_kernel(scale, left_ref, right_ref, out_ref):
+    l1, l2, l3 = pieces(left_ref[...])
+    r1, r2, r3 = pieces(right_ref[...])
+    left = jnp.concatenate([l1, l1, l2, l1, l2, l3], axis=0)
+    right = jnp.concatenate([r1, r2, r1, r3, r2, r1], axis=0)
+    out = lax.dot_general(left, right, (((0,), (0,)), ((), ())), preferred_element_type=F32)
+    out_ref[...] = out * scale
+
+
+def gram_product(left, right, scale):
+    rows, columns = left.shape[1], right.shape[1]
+    tile = 256 if rows % 256 == 0 else rows
+    return pl.pallas_call(
+        functools.partial(gram_kernel, scale),
+        out_shape=jax.ShapeDtypeStruct((rows, columns), F32),
+        grid=(rows // tile,),
+        in_specs=[
+            pl.BlockSpec((left.shape[0], tile), lambda t: (0, t)),
+            pl.BlockSpec(right.shape, lambda t: (0, 0)),
+        ],
+        out_specs=pl.BlockSpec((tile, columns), lambda t: (t, 0)),
+    )(left, right)
 
 
 def body(tokens, cotangent, gate_weight, up_weight, down_weight, model_proj, hidden_proj):
@@ -345,7 +377,7 @@
     left = left.transpose(2, 0, 1, 3).reshape(size, 2 * chunk)
     right = right.transpose(2, 0, 1, 3).reshape(size, -1)
     features = lax.dynamic_slice_in_dim(left, place, 1, 0)
-    gram = jnp.dot(left.T, right, precision=lax.Precision.HIGHEST) / size
+    gram = gram_product(left, right, 1.0 / size)
     return (features, gram)
 
 

time: 449 us -> 449 us (level)
  matrix products: 26 us -> 17 us
  Pallas kernels: 128 us -> 135 us
    dot_general x1 -> x0, matrix products: 8.99 us -> none  [body(): gram = jnp.dot(left.T, right, precision=lax.Precision.HIGHEST) / size]
    pallas_call x0 -> x1, Pallas kernels: none -> 6.83 us  [gram_product(): pl.pallas_call(functools.partial(gram_kernel, scale), out_shape=jax.Shape...]
where the time goes in v2:
time: 449 us; the launch traced here: 448 us
  waiting for transfers between devices  245 us (55%)
  Pallas kernels  135 us (30%)
  starting transfers between devices  17.1 us (4%)
  matrix products  17 us (4%)
  local copies, waits for them, and re-layouts  15.3 us (3%)
  between operations  14.3 us (3%)
    ppermute x24, waiting for transfers between devices, swap(): return lax.ppermute(value, 'ex', [(i, i ^ bit) for i in range(size)])  244 us
    pallas_call x6, Pallas kernels, up_product(): pl.pallas_call(functools.partial(up_kernel, masks, width), out_shape=jax....  74.2 us
    pallas_call x1, Pallas kernels, last_product(): pl.pallas_call(functools.partial(last_kernel, masks, width, dim, len(gate...  18.5 us
    pallas_call x1, Pallas kernels, part_product(): pl.pallas_call(functools.partial(part_kernel, masks, width, dim), out_sha...  18.1 us
    pallas_call x1, Pallas kernels, share(): pl.pallas_call(functools.partial(share_kernel, size, deep), out_shape=[ja...  17.6 us
    ppermute x24, starting transfers between devices, swap(): return lax.ppermute(value, 'ex', [(i, i ^ bit) for i in range(size)])  17.1 us
  transfers between devices with their start and end apart: 26, of which 10 were waited for; matrix products, arithmetic and copies ran while one was open for 6% of the time, Pallas kernels for 21%

profile of v2, /device:TPU:0, one launch (start us, length us, event | category | flops | bytes accessed | tf_op | source)
XLA Modules:
  0.0 447.6 jit_solution(6154501724614673554)
XLA Ops:
  7.2 0.0 all-gather.3.cloned.1.call-start
  7.2 0.7 all-gather.3.cloned.1.call-update
  7.9 0.0 all-gather.5.cloned.1.call-start
  8.0 3.1 collective-permute-start.2
  11.0 23.4 %collective-permute-done.2 = bf16[128,4096]{1,0:T(8,128)(2,1)S(1)} collective-permute-done((bf16[128,4096]{1,0:T(8,128)(2,1)}, bf16[128,4096]{1,0:T(8,128)(2,1)S(1)}, u32[]{:S(2)}, u32[]{:S(2)}) %collective-permute-start.2) | collective-permute-done | bytes 1048608 | tf_op jit(solution)/shard_map/ppermute | solution.py:20
  34.4 2.7 pad_maximum_fusion
  37.2 3.7 constant_dynamic-slice_fusion.4
  40.9 1.7 collective-permute-start.10
  42.7 1.5 collective-permute-start.11
  44.2 0.2 constant_dynamic-slice_fusion.6
  44.4 0.6 collective-permute-start.3
  45.0 0.3 collective-permute-start.4
  45.3 0.2 constant_dynamic-slice_fusion.1
  45.5 0.2 copy-done.3
  45.7 38.2 %collective-permute-done.10.refs_1_ = bf16[1792,512]{1,0:T(8,128)(2,1)} collective-permute-done((bf16[1792,512]{1,0:T(8,128)(2,1)S(1)}, bf16[1792,512]{1,0:T(8,128)(2,1)}, u32[]{:S(2)}, u32[]{:S(2)}) %collective-permute-start.10) | collective-permute-done | bytes 1835040 | tf_op jit(solution)/shard_map/ppermute | solution.py:20
  83.9 1.7 collective-permute-start.15
  85.7 0.2 collective-permute-done.11.refs_2_
  85.9 1.5 collective-permute-start.16
  87.4 35.8 %collective-permute-done.3.refs_1_ = bf16[512,1792]{1,0:T(8,128)(2,1)S(1)} collective-permute-done((bf16[512,1792]{1,0:T(8,128)(2,1)S(1)}, bf16[512,1792]{1,0:T(8,128)(2,1)S(1)}, u32[]{:S(2)}, u32[]{:S(2)}) %collective-permute-start.3) | collective-permute-done | bytes 1835040 | tf_op jit(solution)/shard_map/ppermute | solution.py:20
  123.1 2.0 collective-permute-done.4.refs_2_
  125.1 1.5 collective-permute-start.5
  126.6 0.1 collective-permute-start.7
  126.7 34.3 %collective-permute-done.15.refs_1_ = bf16[512,1792]{1,0:T(8,128)(2,1)} collective-permute-done((bf16[512,1792]{1,0:T(8,128)(2,1)S(1)}, bf16[512,1792]{1,0:T(8,128)(2,1)}, u32[]{:S(2)}, u32[]{:S(2)}) %collective-permute-start.15) | collective-permute-done | bytes 1835040 | tf_op jit(solution)/shard_map/ppermute | solution.py:20
  161.0 3.6 collective-permute-done.16.refs_2_
  164.5 1.5 collective-permute-start.17
  166.0 0.1 collective-permute-start.19
  166.1 37.7 %collective-permute-done.5.refs_3_ = bf16[512,1792]{1,0:T(8,128)(2,1)} collective-permute-done((bf16[512,1792]{1,0:T(8,128)(2,1)S(1)}, bf16[512,1792]{1,0:T(8,128)(2,1)}, u32[]{:S(2)}, u32[]{:S(2)}) %collective-permute-start.5) | collective-permute-done | bytes 1835040 | tf_op jit(solution)/shard_map/ppermute | solution.py:20
  203.9 1.6 collective-permute-start.22
  205.4 0.3 collective-permute-start.9
  205.7 37.5 %collective-permute-done.17.refs_3_ = bf16[512,1792]{1,0:T(8,128)(2,1)} collective-permute-done((bf16[512,1792]{1,0:T(8,128)(2,1)}, bf16[512,1792]{1,0:T(8,128)(2,1)}, u32[]{:S(2)}, u32[]{:S(2)}) %collective-permute-start.17) | collective-permute-done | bytes 1835040 | tf_op jit(solution)/shard_map/ppermute | solution.py:20
  243.2 0.0 all-gather.3.cloned.1.call-done.x_ref
  243.2 4.7 %fusion.22 = (bf16[256,4096]{1,0:T(8,128)(2,1)}, bf16[256,4096]{1,0:T(8,128)(2,1)}) fusion(bf16[512,4096]{1,0:T(8,128)(2,1)} %all-gather.3.cloned.1.call-done.x_ref), kind=kLoop, calls=%fused_computation.36 | loop fusion | bytes 8388608 | tf_op jit(solution)/shard_map/slice | solution.py:340
  247.9 0.3 collective-permute-start.1
  248.2 0.3 collective-permute-start.12
  248.5 31.8 %collective-permute-done.22.refs_6_ = bf16[1792,512]{1,0:T(8,128)(2,1)} collective-permute-done((bf16[1792,512]{1,0:T(8,128)(2,1)}, bf16[1792,512]{1,0:T(8,128)(2,1)}, u32[]{:S(2)}, u32[]{:S(2)}) %collective-permute-start.22) | collective-permute-done | bytes 1835040 | tf_op jit(solution)/shard_map/ppermute | solution.py:20
  280.3 0.5 collective-permute-start.14
  280.8 0.6 collective-permute-start
  281.4 1.2 constant_dynamic-slice_fusion.3.proj_ref
  282.6 14.4 %shard_map.86.refs_3_ = f32[512,1792]{1,0:T(8,128)} custom-call(s32[1]{0:T(128)} %bitcast.place_ref, bf16[512,4096]{1,0:T(8,128)(2,1)} %all-gather.3.cloned.1.call-done.x_ref, bf16[512,1792]{1,0:T(8,128)(2,1)} %copy-done.3, bf16[512,1792]{1,0:T(8,128)(2,1)} %copy-done.5, bf16[512,1792]{1,0:T(8,128)(2,1)} %copy-done.6, ...), custom_call_target="tpu_custom_call" | custom-call | tf_op jit(solution)/shard_map/pallas_call | solution.py:52
  297.1 14.5 %shard_map.89.refs_0_ = f32[512,1792]{1,0:T(8,128)} custom-call(s32[1]{0:T(128)} %bitcast.place_ref, bf16[512,4096]{1,0:T(8,128)(2,1)} %all-gather.3.cloned.1.call-done.x_ref, bf16[512,1792]{1,0:T(8,128)(2,1)} %copy-done.4, bf16[512,1792]{1,0:T(8,128)(2,1)} %collective-permute-done.15.refs_1_, bf16[512,1792]{1,0:T(8,128)(2,1)} %collective-permute-done.16.refs_2_, ...), custom_call_target="tpu_custom_call" | custom-call | tf_op jit(solution)/shard_map/pallas_call | solution.py:52
  311.5 0.1 collective-permute-start.23
  311.6 3.6 fusion.11
  315.2 11.4 %shard_map.87.refs_4_ = f32[256,1792]{1,0:T(8,128)} custom-call(s32[1]{0:T(128)} %bitcast.place_ref, bf16[256,4096]{1,0:T(8,128)(2,1)} %collective-permute-done.1.x_ref, bf16[512,1792]{1,0:T(8,128)(2,1)} %copy-done.3, bf16[512,1792]{1,0:T(8,128)(2,1)} %copy-done.5, bf16[512,1792]{1,0:T(8,128)(2,1)} %copy-done.6, ...), custom_call_target="tpu_custom_call" | custom-call | tf_op jit(solution)/shard_map/pallas_call | solution.py:52
  326.6 11.3 %shard_map.90.refs_1_ = f32[256,1792]{1,0:T(8,128)} custom-call(s32[1]{0:T(128)} %bitcast.place_ref, bf16[256,4096]{1,0:T(8,128)(2,1)} %collective-permute-done.1.x_ref, bf16[512,1792]{1,0:T(8,128)(2,1)} %copy-done.4, bf16[512,1792]{1,0:T(8,128)(2,1)} %collective-permute-done.15.refs_1_, bf16[512,1792]{1,0:T(8,128)(2,1)} %collective-permute-done.16.refs_2_, ...), custom_call_target="tpu_custom_call" | custom-call | tf_op jit(solution)/shard_map/pallas_call | solution.py:52
  337.9 2.3 fusion.9
  340.3 0.0 all-gather.5.cloned.1.call-done.y_ref
  340.3 18.1 %shard_map.88.part_ref = f32[1024,1792]{1,0:T(8,128)} custom-call(s32[1]{0:T(128)} %bitcast.place_ref, bf16[512,8192]{1,0:T(8,128)(2,1)} %all-gather.5.cloned.1.call-done.y_ref, bf16[1792,512]{1,0:T(8,128)(2,1)} %get-tuple-element.31.refs_0_, bf16[1792,512]{1,0:T(8,128)(2,1)} %collective-permute-done.10.refs_1_, ...), custom_call_target="tpu_custom_call" | custom-call | tf_op jit(solution)/shard_map/pallas_call | solution.py:92
  358.4 4.1 fusion
  362.4 0.6 copy-done.2
  363.0 1.7 fusion.2
  364.8 11.4 %shard_map.92.refs_5_ = f32[256,1792]{1,0:T(8,128)} custom-call(s32[1]{0:T(128)} %bitcast.place_ref, bf16[256,4096]{1,0:T(8,128)(2,1)} %collective-permute-done.x_ref, bf16[512,1792]{1,0:T(8,128)(2,1)} %copy-done.3, bf16[512,1792]{1,0:T(8,128)(2,1)} %copy-done.5, bf16[512,1792]{1,0:T(8,128)(2,1)} %copy-done.6, ...), custom_call_target="tpu_custom_call" | custom-call | tf_op jit(solution)/shard_map/pallas_call | solution.py:52
  376.1 11.3 %shard_map.91.refs_2_ = f32[256,1792]{1,0:T(8,128)} custom-call(s32[1]{0:T(128)} %bitcast.place_ref, bf16[256,4096]{1,0:T(8,128)(2,1)} %collective-permute-done.x_ref, bf16[512,1792]{1,0:T(8,128)(2,1)} %copy-done.4, bf16[512,1792]{1,0:T(8,128)(2,1)} %collective-permute-done.15.refs_1_, bf16[512,1792]{1,0:T(8,128)(2,1)} %collective-permute-done.16.refs_2_, ...), custom_call_target="tpu_custom_call" | custom-call | tf_op jit(solution)/shard_map/pallas_call | solution.py:52
  387.4 2.3 fusion.7
  389.8 18.5 %shard_map.93 = (f32[1024,128]{1,0:T(8,128)}, f32[1024,128]{1,0:T(8,128)}) custom-call(s32[1]{0:T(128)} %bitcast.place_ref, bf16[512,8192]{1,0:T(8,128)(2,1)} %all-gather.5.cloned.1.call-done.y_ref, f32[1024,1792]{1,0:T(8,128)} %shard_map.88.part_ref, bf16[1792,384]{1,0:T(8,128)(2,1)} %constant_dynamic-slice_fusion.3.proj_ref, ...), custom_call_target="tpu_custom_call" | custom-call | tf_op jit(solution)/shard_map/pallas_call | solution.py:138
  408.3 1.5 fusion.16
  409.8 1.5 fusion.4
  411.3 0.7 maximum_bitcast_fusion.1.part_ref
  412.0 17.6 %shard_map.94 = (f32[4,2,2,1024]{3,2,1,0:T(2,128)}, f32[4,1,2,1024]{3,2,1,0:T(2,128)}) custom-call(f32[8,2,1024]{2,1,0:T(2,128)} %maximum_bitcast_fusion.1.part_ref), custom_call_target="tpu_custom_call" | custom-call | tf_op jit(solution)/shard_map/pallas_call | solution.py:263
  429.5 0.9 copy.9
  430.4 0.7 copy.11
  431.0 0.8 copy.10
  431.8 0.6 reshape.77.right_ref
  432.5 6.8 %shard_map.95 = f32[2048,1024]{1,0:T(8,128)} custom-call(f32[8,2048]{1,0:T(8,128)} %bitcast.27, f32[8,1024]{1,0:T(8,128)} %reshape.77.right_ref), custom_call_target="tpu_custom_call" | custom-call | tf_op jit(solution)/shard_map/pallas_call | solution.py:305
  439.3 1.4 constant_dynamic-slice_fusion
  (49 shorter events, 0.1 us)
Async XLA Ops:
  7.2 274.2 %copy-start = (bf16[3584,384]{1,0:T(8,128)(2,1)S(1)}, bf16[3584,384]{1,0:T(8,128)(2,1)}, u32[]{:S(2)}) copy-start(bf16[3584,384]{1,0:T(8,128)(2,1)} %param.13) | copy-start | bytes 8257540
  7.2 236.0 %all-gather.3.cloned.1.call-start = ((), (), s32[]{:S(2)}) async-start(), calls=%async_computation | async-start | bytes 5242880 | tf_op jit(solution)/shard_map/all_gather | solution.py:334
  7.9 332.4 %all-gather.5.cloned.1.call-start = ((), (), s32[]{:S(2)}) async-start(), calls=%async_computation.1 | async-start | bytes 10485760 | tf_op jit(solution)/shard_map/all_gather | solution.py:336
  8.0 26.4 %collective-permute-start.2 = (bf16[128,4096]{1,0:T(8,128)(2,1)}, bf16[128,4096]{1,0:T(8,128)(2,1)S(1)}, u32[]{:S(2)}, u32[]{:S(2)}) collective-permute-start(bf16[128,4096]{1,0:T(8,128)(2,1)} %param.8), channel_id=1, source_target_pairs={{0,16},{4,20},{8,24},{12,28},{16,0},{20,4},{24,8},{28,12},{1,17},{... | collective-permute-start | bytes 3145736 | tf_op jit(solution)/shard_map/ppermute | solution.py:20
  37.2 7.0 %copy-start.12 = (bf16[512,3584]{1,0:T(8,128)(2,1)S(1)}, bf16[512,3584]{1,0:T(8,128)(2,1)}, u32[]{:S(2)}) copy-start(bf16[512,3584]{1,0:T(8,128)(2,1)} %param.10) | copy-start | bytes 11010052
  40.9 43.0 %collective-permute-start.10 = (bf16[1792,512]{1,0:T(8,128)(2,1)S(1)}, bf16[1792,512]{1,0:T(8,128)(2,1)}, u32[]{:S(2)}, u32[]{:S(2)}) collective-permute-start(bf16[1792,512]{1,0:T(8,128)(2,1)S(1)} %get-tuple-element.30), channel_id=1, source_target_pairs={{0,16},{4,20},{8,24},{12,28},{16,0},{20,4},{24,8},{28,12},{1,17},{... | collective-permute-start | bytes 5505032 | tf_op jit(solution)/shard_map/ppermute | solution.py:20
  42.7 2.6 copy-start.13
  42.7 43.2 %collective-permute-start.11 = (bf16[1792,512]{1,0:T(8,128)(2,1)}, bf16[1792,512]{1,0:T(8,128)(2,1)}, u32[]{:S(2)}, u32[]{:S(2)}) collective-permute-start(bf16[1792,512]{1,0:T(8,128)(2,1)} %get-tuple-element.31.refs_0_), channel_id=1, source_target_pairs={{0,8},{4,12},{8,0},{12,4},{16,24},{20,28},{24,16},{28,20},{1,9},{5... | collective-permute-start | bytes 5505032 | tf_op jit(solution)/shard_map/ppermute | solution.py:20
  44.4 1.3 copy-start.3
  44.4 78.7 %collective-permute-start.3 = (bf16[512,1792]{1,0:T(8,128)(2,1)S(1)}, bf16[512,1792]{1,0:T(8,128)(2,1)S(1)}, u32[]{:S(2)}, u32[]{:S(2)}) collective-permute-start(bf16[512,1792]{1,0:T(8,128)(2,1)S(1)} %get-tuple-element.32), channel_id=1, source_target_pairs={{0,16},{4,20},{8,24},{12,28},{16,0},{20,4},{24,8},{28,12},{1,17},{... | collective-permute-start | bytes 5505032 | tf_op jit(solution)/shard_map/ppermute | solution.py:20
  45.0 80.1 %collective-permute-start.4 = (bf16[512,1792]{1,0:T(8,128)(2,1)S(1)}, bf16[512,1792]{1,0:T(8,128)(2,1)S(1)}, u32[]{:S(2)}, u32[]{:S(2)}) collective-permute-start(bf16[512,1792]{1,0:T(8,128)(2,1)S(1)} %get-tuple-element.33.refs_0_), channel_id=1, source_target_pairs={{0,8},{4,12},{8,0},{12,4},{16,24},{20,28},{24,16},{28,20},{1,9},{5... | collective-permute-start | bytes 5505032 | tf_op jit(solution)/shard_map/ppermute | solution.py:20
  45.3 81.3 %collective-permute-start.6 = (bf16[512,1792]{1,0:T(8,128)(2,1)S(1)}, bf16[512,1792]{1,0:T(8,128)(2,1)S(1)}, u32[]{:S(2)}, u32[]{:S(2)}) collective-permute-start(bf16[512,1792]{1,0:T(8,128)(2,1)S(1)} %get-tuple-element.33.refs_0_), channel_id=1, source_target_pairs={{0,4},{4,0},{8,12},{12,8},{16,20},{20,16},{24,28},{28,24},{1,5},{5... | collective-permute-start | bytes 5505032 | tf_op jit(solution)/shard_map/ppermute | solution.py:20
  45.7 80.9 %copy-start.4 = (bf16[512,1792]{1,0:T(8,128)(2,1)}, bf16[512,1792]{1,0:T(8,128)(2,1)S(1)}, u32[]{:S(2)}) copy-start(bf16[512,1792]{1,0:T(8,128)(2,1)S(1)} %get-tuple-element.29.refs_0_) | copy-start | bytes 5505028
  83.9 77.0 %collective-permute-start.15 = (bf16[512,1792]{1,0:T(8,128)(2,1)S(1)}, bf16[512,1792]{1,0:T(8,128)(2,1)}, u32[]{:S(2)}, u32[]{:S(2)}) collective-permute-start(bf16[512,1792]{1,0:T(8,128)(2,1)S(1)} %get-tuple-element.28), channel_id=1, source_target_pairs={{0,16},{4,20},{8,24},{12,28},{16,0},{20,4},{24,8},{28,12},{1,17},{... | collective-permute-start | bytes 5505032 | tf_op jit(solution)/shard_map/ppermute | solution.py:20
  85.9 78.6 %collective-permute-start.16 = (bf16[512,1792]{1,0:T(8,128)(2,1)S(1)}, bf16[512,1792]{1,0:T(8,128)(2,1)}, u32[]{:S(2)}, u32[]{:S(2)}) collective-permute-start(bf16[512,1792]{1,0:T(8,128)(2,1)S(1)} %get-tuple-element.29.refs_0_), channel_id=1, source_target_pairs={{0,8},{4,12},{8,0},{12,4},{16,24},{20,28},{24,16},{28,20},{1,9},{5... | collective-permute-start | bytes 5505032 | tf_op jit(solution)/shard_map/ppermute | solution.py:20
  123.1 42.9 %copy-start.5 = (bf16[512,1792]{1,0:T(8,128)(2,1)}, bf16[512,1792]{1,0:T(8,128)(2,1)S(1)}, u32[]{:S(2)}) copy-start(bf16[512,1792]{1,0:T(8,128)(2,1)S(1)} %collective-permute-done.3.refs_1_) | copy-start | bytes 5505028
  123.1 42.9 %collective-permute-start.18 = (bf16[512,1792]{1,0:T(8,128)(2,1)S(1)}, bf16[512,1792]{1,0:T(8,128)(2,1)S(1)}, u32[]{:S(2)}, u32[]{:S(2)}) collective-permute-start(bf16[512,1792]{1,0:T(8,128)(2,1)S(1)} %get-tuple-element.29.refs_0_), channel_id=1, source_target_pairs={{0,4},{4,0},{8,12},{12,8},{16,20},{20,16},{24,28},{28,24},{1,5},{5... | collective-permute-start | bytes 5505032 | tf_op jit(solution)/shard_map/ppermute | solution.py:20
  125.1 78.8 %copy-start.6 = (bf16[512,1792]{1,0:T(8,128)(2,1)}, bf16[512,1792]{1,0:T(8,128)(2,1)S(1)}, u32[]{:S(2)}) copy-start(bf16[512,1792]{1,0:T(8,128)(2,1)S(1)} %collective-permute-done.4.refs_2_) | copy-start | bytes 5505028
  125.1 78.8 %collective-permute-start.5 = (bf16[512,1792]{1,0:T(8,128)(2,1)S(1)}, bf16[512,1792]{1,0:T(8,128)(2,1)}, u32[]{:S(2)}, u32[]{:S(2)}) collective-permute-start(bf16[512,1792]{1,0:T(8,128)(2,1)S(1)} %collective-permute-done.3.refs_1_), channel_id=1, source_target_pairs={{0,8},{4,12},{8,0},{12,4},{16,24},{20,28},{24,16},{28,20},{1,9},{5... | collective-permute-start | bytes 5505032 | tf_op jit(solution)/shard_map/ppermute | solution.py:20
  126.6 78.8 %copy-start.7 = (bf16[512,1792]{1,0:T(8,128)(2,1)}, bf16[512,1792]{1,0:T(8,128)(2,1)S(1)}, u32[]{:S(2)}) copy-start(bf16[512,1792]{1,0:T(8,128)(2,1)S(1)} %collective-permute-done.6.refs_4_) | copy-start | bytes 5505028
  126.6 77.3 %collective-permute-start.7 = (bf16[512,1792]{1,0:T(8,128)(2,1)S(1)}, bf16[512,1792]{1,0:T(8,128)(2,1)S(1)}, u32[]{:S(2)}, u32[]{:S(2)}) collective-permute-start(bf16[512,1792]{1,0:T(8,128)(2,1)S(1)} %collective-permute-done.3.refs_1_), channel_id=1, source_target_pairs={{0,4},{4,0},{8,12},{12,8},{16,20},{20,16},{24,28},{28,24},{1,5},{5... | collective-permute-start | bytes 5505032 | tf_op jit(solution)/shard_map/ppermute | solution.py:20
  161.0 44.5 %collective-permute-start.8 = (bf16[512,1792]{1,0:T(8,128)(2,1)S(1)}, bf16[512,1792]{1,0:T(8,128)(2,1)S(1)}, u32[]{:S(2)}, u32[]{:S(2)}) collective-permute-start(bf16[512,1792]{1,0:T(8,128)(2,1)S(1)} %collective-permute-done.4.refs_2_), channel_id=1, source_target_pairs={{0,4},{4,0},{8,12},{12,8},{16,20},{20,16},{24,28},{28,24},{1,5},{5... | collective-permute-start | bytes 5505032 | tf_op jit(solution)/shard_map/ppermute | solution.py:20
  164.5 78.6 %collective-permute-start.17 = (bf16[512,1792]{1,0:T(8,128)(2,1)}, bf16[512,1792]{1,0:T(8,128)(2,1)}, u32[]{:S(2)}, u32[]{:S(2)}) collective-permute-start(bf16[512,1792]{1,0:T(8,128)(2,1)} %collective-permute-done.15.refs_1_), channel_id=1, source_target_pairs={{0,8},{4,12},{8,0},{12,4},{16,24},{20,28},{24,16},{28,20},{1,9},{5... | collective-permute-start | bytes 5505032 | tf_op jit(solution)/shard_map/ppermute | solution.py:20
  166.0 39.7 %copy-start.8 = (bf16[512,1792]{1,0:T(8,128)(2,1)}, bf16[512,1792]{1,0:T(8,128)(2,1)S(1)}, u32[]{:S(2)}) copy-start(bf16[512,1792]{1,0:T(8,128)(2,1)S(1)} %collective-permute-done.18.refs_4_) | copy-start | bytes 5505028
  166.0 81.9 %collective-permute-start.19 = (bf16[512,1792]{1,0:T(8,128)(2,1)}, bf16[512,1792]{1,0:T(8,128)(2,1)}, u32[]{:S(2)}, u32[]{:S(2)}) collective-permute-start(bf16[512,1792]{1,0:T(8,128)(2,1)} %collective-permute-done.15.refs_1_), channel_id=1, source_target_pairs={{0,4},{4,0},{8,12},{12,8},{16,20},{20,16},{24,28},{28,24},{1,5},{5... | collective-permute-start | bytes 5505032 | tf_op jit(solution)/shard_map/ppermute | solution.py:20
  203.8 44.4 %collective-permute-start.20 = (bf16[512,1792]{1,0:T(8,128)(2,1)}, bf16[512,1792]{1,0:T(8,128)(2,1)}, u32[]{:S(2)}, u32[]{:S(2)}) collective-permute-start(bf16[512,1792]{1,0:T(8,128)(2,1)} %collective-permute-done.16.refs_2_), channel_id=1, source_target_pairs={{0,4},{4,0},{8,12},{12,8},{16,20},{20,16},{24,28},{28,24},{1,5},{5... | collective-permute-start | bytes 5505032 | tf_op jit(solution)/shard_map/ppermute | solution.py:20
  203.9 39.3 %copy-start.9 = (bf16[512,1792]{1,0:T(8,128)(2,1)}, bf16[512,1792]{1,0:T(8,128)(2,1)S(1)}, u32[]{:S(2)}) copy-start(bf16[512,1792]{1,0:T(8,128)(2,1)S(1)} %collective-permute-done.7.refs_5_) | copy-start | bytes 5505028
  203.9 76.5 %collective-permute-start.22 = (bf16[1792,512]{1,0:T(8,128)(2,1)}, bf16[1792,512]{1,0:T(8,128)(2,1)}, u32[]{:S(2)}, u32[]{:S(2)}) collective-permute-start(bf16[1792,512]{1,0:T(8,128)(2,1)} %collective-permute-done.10.refs_1_), channel_id=1, source_target_pairs={{0,8},{4,12},{8,0},{12,4},{16,24},{20,28},{24,16},{28,20},{1,9},{5... | collective-permute-start | bytes 5505032 | tf_op jit(solution)/shard_map/ppermute | solution.py:20
  205.4 37.7 %copy-start.10 = (bf16[512,1792]{1,0:T(8,128)(2,1)}, bf16[512,1792]{1,0:T(8,128)(2,1)S(1)}, u32[]{:S(2)}) copy-start(bf16[512,1792]{1,0:T(8,128)(2,1)S(1)} %collective-permute-done.8.refs_6_) | copy-start | bytes 5505028
  205.4 74.9 %collective-permute-start.9 = (bf16[512,1792]{1,0:T(8,128)(2,1)}, bf16[512,1792]{1,0:T(8,128)(2,1)}, u32[]{:S(2)}, u32[]{:S(2)}) collective-permute-start(bf16[512,1792]{1,0:T(8,128)(2,1)} %collective-permute-done.5.refs_3_), channel_id=1, source_target_pairs={{0,4},{4,0},{8,12},{12,8},{16,20},{20,16},{24,28},{28,24},{1,5},{5... | collective-permute-start | bytes 5505032 | tf_op jit(solution)/shard_map/ppermute | solution.py:20
  243.2 37.7 %collective-permute-start.21 = (bf16[512,1792]{1,0:T(8,128)(2,1)}, bf16[512,1792]{1,0:T(8,128)(2,1)}, u32[]{:S(2)}, u32[]{:S(2)}) collective-permute-start(bf16[512,1792]{1,0:T(8,128)(2,1)} %collective-permute-done.17.refs_3_), channel_id=1, source_target_pairs={{0,4},{4,0},{8,12},{12,8},{16,20},{20,16},{24,28},{28,24},{1,5},{5... | collective-permute-start | bytes 5505032 | tf_op jit(solution)/shard_map/ppermute | solution.py:20
  247.9 63.6 %collective-permute-start.1 = (bf16[256,4096]{1,0:T(8,128)(2,1)}, bf16[256,4096]{1,0:T(8,128)(2,1)}, u32[]{:S(2)}, u32[]{:S(2)}) collective-permute-start(bf16[256,4096]{1,0:T(8,128)(2,1)} %get-tuple-element.26), channel_id=1, source_target_pairs={{0,16},{4,20},{8,24},{12,28},{16,0},{20,4},{24,8},{28,12},{1,17},{... | collective-permute-start | bytes 6291464 | tf_op jit(solution)/shard_map/ppermute | solution.py:20
  248.2 92.0 %collective-permute-start.12 = (bf16[1792,512]{1,0:T(8,128)(2,1)}, bf16[1792,512]{1,0:T(8,128)(2,1)}, u32[]{:S(2)}, u32[]{:S(2)}) collective-permute-start(bf16[1792,512]{1,0:T(8,128)(2,1)} %get-tuple-element.31.refs_0_), channel_id=1, source_target_pairs={{0,4},{4,0},{8,12},{12,8},{16,20},{20,16},{24,28},{28,24},{1,5},{5... | collective-permute-start | bytes 5505032 | tf_op jit(solution)/shard_map/ppermute | solution.py:20
  280.3 59.9 %collective-permute-start.13 = (bf16[1792,512]{1,0:T(8,128)(2,1)}, bf16[1792,512]{1,0:T(8,128)(2,1)}, u32[]{:S(2)}, u32[]{:S(2)}) collective-permute-start(bf16[1792,512]{1,0:T(8,128)(2,1)} %collective-permute-done.10.refs_1_), channel_id=1, source_target_pairs={{0,4},{4,0},{8,12},{12,8},{16,20},{20,16},{24,28},{28,24},{1,5},{5... | collective-permute-start | bytes 5505032 | tf_op jit(solution)/shard_map/ppermute | solution.py:20
  280.3 59.9 %collective-permute-start.14 = (bf16[1792,512]{1,0:T(8,128)(2,1)}, bf16[1792,512]{1,0:T(8,128)(2,1)}, u32[]{:S(2)}, u32[]{:S(2)}) collective-permute-start(bf16[1792,512]{1,0:T(8,128)(2,1)} %collective-permute-done.11.refs_2_), channel_id=1, source_target_pairs={{0,4},{4,0},{8,12},{12,8},{16,20},{20,16},{24,28},{28,24},{1,5},{5... | collective-permute-start | bytes 5505032 | tf_op jit(solution)/shard_map/ppermute | solution.py:20
  280.8 83.9 %collective-permute-start = (bf16[256,4096]{1,0:T(8,128)(2,1)}, bf16[256,4096]{1,0:T(8,128)(2,1)}, u32[]{:S(2)}, u32[]{:S(2)}) collective-permute-start(bf16[256,4096]{1,0:T(8,128)(2,1)} %get-tuple-element.27), channel_id=1, source_target_pairs={{0,16},{4,20},{8,24},{12,28},{16,0},{20,4},{24,8},{28,12},{1,17},{... | collective-permute-start | bytes 6291464 | tf_op jit(solution)/shard_map/ppermute | solution.py:20
  297.1 14.6 %copy-start.11 = (bf16[4096,128]{1,0:T(8,128)(2,1)S(1)}, bf16[4096,128]{1,0:T(8,128)(2,1)}, u32[]{:S(2)}) copy-start(bf16[4096,128]{1,0:T(8,128)(2,1)} %param.12) | copy-start | bytes 3145732
  311.5 78.3 %collective-permute-start.23 = (bf16[1792,512]{1,0:T(8,128)(2,1)}, bf16[1792,512]{1,0:T(8,128)(2,1)}, u32[]{:S(2)}, u32[]{:S(2)}) collective-permute-start(bf16[1792,512]{1,0:T(8,128)(2,1)} %collective-permute-done.22.refs_6_), channel_id=1, source_target_pairs={{0,4},{4,0},{8,12},{12,8},{16,20},{20,16},{24,28},{28,24},{1,5},{5... | collective-permute-start | bytes 5505032 | tf_op jit(solution)/shard_map/ppermute | solution.py:20
  358.4 4.6 %copy-start.2 = (bf16[512,8192]{1,0:T(8,128)(2,1)S(1)}, bf16[512,8192]{1,0:T(8,128)(2,1)}, u32[]{:S(2)}) copy-start(bf16[512,8192]{1,0:T(8,128)(2,1)} %all-gather.5.cloned.1.call-done.y_ref) | copy-start | bytes 25165828
  432.4 8.3 %copy-start.1 = (bf16[3584,384]{1,0:T(8,128)(2,1)S(1)}, bf16[3584,384]{1,0:T(8,128)(2,1)}, u32[]{:S(2)}) copy-start(bf16[3584,384]{1,0:T(8,128)(2,1)} %param.13) | copy-start | bytes 8257540
Sparse Core Ops, SparseCore 0:
  9.6 83.4 all-gather.2
  95.2 148.0 all-gather.4

commit v3 on v2

--- a/solution.py
+++ b/solution.py
@@ -107,15 +107,14 @@
     gates, ups = refs[:groups], refs[groups : 2 * groups]
     *blocks, b_ref, g_ref = refs[2 * groups :]
     own, other = down_dots(masks, width, dim, place_ref, y_ref, blocks)
-    count = y_ref.shape[0]
+    fresh = jnp.concatenate([own, other], axis=0)
     first = pl.program_id(0) == 0
     at = 0
     for gate_ref, up_ref in zip(gates, ups):
         gate = gate_ref[...]
         up = up_ref[...]
         rows = gate.shape[0]
-        fresh = own[at : at + rows] if at < count else other[at - count : at - count + rows]
-        grad = part_ref[at : at + rows] + fresh
+        grad = part_ref[at : at + rows] + fresh[at : at + rows]
         sig = jax.nn.sigmoid(gate)
         active = gate * sig
         hidden = (active * up).astype(jnp.bfloat16)
@@ -337,30 +336,32 @@
     dim = in_own.shape[1]
     split = in_own.shape[0] // 2
     ins = {
-        "own": in_own, "0": swap(in_own[:split], top, size), "1": swap(in_own[split:], top, size)
+        "0": jnp.concatenate([in_own, swap(in_own[:split], top, size)], axis=0),
+        "1": swap(in_own[split:], top, size),
     }
 
     gates = spread(gate_mine, swap(gate_theirs, top, size), top, size)
     ups = spread(up_mine, swap(up_theirs, top, size), top, size)
-    downs = spread(down_mine, swap(down_theirs, top, size), top, size)
+    first_in = jnp.dot(ins["0"], model_proj[:, :KA], preferred_element_type=F32)
+    ins["0"], first_in = lax.optimization_barrier((ins["0"], first_in))
+    down_crossed = swap(down_theirs, top, size)
+    downs = spread(down_mine, down_crossed, top, size)
 
     where = place.astype(jnp.int32).reshape(1)
     late = top | (top // 2)
     part = part_product(cot_both, [h for h in downs if h[0] & late != late], where)
-    gate, up, proj_in = [], [], []
+    gate, up = [], []
     proj_cot = [
         jnp.dot(cot_both[:, k * dim : (k + 1) * dim], model_proj[:, KA:], preferred_element_type=F32)
         for k in range(2)
     ]
     for name, rows in ins.items():
         if name == "1":
-            rows, proj_in, proj_cot, up, part = lax.optimization_barrier(
-                (rows, proj_in, proj_cot, up, part)
-            )
+            rows, proj_cot, up, part = lax.optimization_barrier((rows, proj_cot, up, part))
         gate.append(up_product(rows, gates, where))
         up.append(up_product(rows, ups, where))
-        proj_in.append(jnp.dot(rows, model_proj[:, :KA], preferred_element_type=F32))
-    proj_in = [proj_in[0], jnp.concatenate(proj_in[1:], axis=0)]
+    last_in = jnp.dot(rows, model_proj[:, :KA], preferred_element_type=F32)
+    proj_in = [first_in[: 2 * split], jnp.concatenate([first_in[2 * split :], last_in], axis=0)]
     hp = lax.dynamic_slice_in_dim(hidden_proj, side * half, half, 0)
     proj_hidden, proj_grad = last_product(
         cot_both, part, gate, up, hp, [h for h in downs if h[0] & late == late], where

time: 449 us -> 445 us (level)
  Pallas kernels: 135 us -> 118 us
  waiting for transfers between devices: 245 us -> 257 us
  local copies, waits for them, and re-layouts: 15.3 us -> 21.6 us
  matrix products: 17 us -> 11.9 us
    pallas_call x6 -> x4, Pallas kernels: 74.2 us -> 58.2 us  [up_product(): pl.pallas_call(functools.partial(up_kernel, masks, width), out_shape=jax....]
    ppermute x24, waiting for transfers between devices: 244 us -> 256 us  [swap(): return lax.ppermute(value, 'ex', [(i, i ^ bit) for i in range(size)])]
    dot_general x3 -> x2, matrix products: 8.28 us -> 2.82 us  [the longest x1 2.06 us: body(): first_in = jnp.dot(ins['0'], model_proj[:, :KA], preferred_element_type=F32)]
    unnamed x29 -> x42, local copies, waits for them, and re-layouts: 1.45 us -> 6.07 us
  transfers between devices with their start and end apart: 26 -> 26, of which waited for: 10 -> 11; matrix products, arithmetic and copies ran while one was open for 6% -> 6% of each run, Pallas kernels for 21% -> 17%
where the time goes in v3:
time: 445 us; the launch traced here: 443 us
  waiting for transfers between devices  257 us (58%)
  Pallas kernels  118 us (27%)
  local copies, waits for them, and re-layouts  21.6 us (5%)
  starting transfers between devices  17.1 us (4%)
  between operations  14.3 us (3%)
  matrix products  11.9 us (3%)
    ppermute x24, waiting for transfers between devices, swap(): return lax.ppermute(value, 'ex', [(i, i ^ bit) for i in range(size)])  256 us
    pallas_call x4, Pallas kernels, up_product(): pl.pallas_call(functools.partial(up_kernel, masks, width), out_shape=jax....  58.2 us
    pallas_call x1, Pallas kernels, last_product(): pl.pallas_call(functools.partial(last_kernel, masks, width, dim, len(gate...  18.3 us
    pallas_call x1, Pallas kernels, part_product(): pl.pallas_call(functools.partial(part_kernel, masks, width, dim), out_sha...  18.1 us
    ppermute x24, starting transfers between devices, swap(): return lax.ppermute(value, 'ex', [(i, i ^ bit) for i in range(size)])  17 us
    pallas_call x1, Pallas kernels, share(): pl.pallas_call(functools.partial(share_kernel, size, deep), out_shape=[ja...  16.6 us
  transfers between devices with their start and end apart: 26, of which 11 were waited for; matrix products, arithmetic and copies ran while one was open for 6% of the time, Pallas kernels for 17%

profile of v3, /device:TPU:0, one launch (start us, length us, event | category | flops | bytes accessed | tf_op | source)
XLA Modules:
  0.0 443.4 jit_solution(1606317453623093628)
XLA Ops:
  7.2 0.0 all-gather.3.cloned.1.call-start
  7.2 0.7 all-gather.3.cloned.1.call-update
  7.9 0.0 all-gather.5.cloned.1.call-start
  8.0 3.1 collective-permute-start.2
  11.0 23.4 %collective-permute-done.2 = bf16[128,4096]{1,0:T(8,128)(2,1)S(1)} collective-permute-done((bf16[128,4096]{1,0:T(8,128)(2,1)}, bf16[128,4096]{1,0:T(8,128)(2,1)S(1)}, u32[]{:S(2)}, u32[]{:S(2)}) %collective-permute-start.2) | collective-permute-done | bytes 1048608 | tf_op jit(solution)/shard_map/ppermute | solution.py:20
  34.4 2.8 pad_maximum_fusion
  37.2 3.7 constant_dynamic-slice_fusion.4
  41.0 1.7 collective-permute-start.10
  42.7 1.5 collective-permute-start.11
  44.2 0.2 constant_dynamic-slice_fusion.6
  44.5 0.6 collective-permute-start.3
  45.0 0.3 collective-permute-start.4
  45.3 0.2 constant_dynamic-slice_fusion.1
  45.6 0.1 copy-done.6
  45.7 38.2 %collective-permute-done.10.refs_1_ = bf16[1792,512]{1,0:T(8,128)(2,1)} collective-permute-done((bf16[1792,512]{1,0:T(8,128)(2,1)S(1)}, bf16[1792,512]{1,0:T(8,128)(2,1)}, u32[]{:S(2)}, u32[]{:S(2)}) %collective-permute-start.10) | collective-permute-done | bytes 1835040 | tf_op jit(solution)/shard_map/ppermute | solution.py:20
  84.0 1.7 collective-permute-start.15
  85.7 0.2 collective-permute-done.11.refs_2_
  85.9 1.5 collective-permute-start.16
  87.4 35.8 %collective-permute-done.3.refs_1_ = bf16[512,1792]{1,0:T(8,128)(2,1)S(1)} collective-permute-done((bf16[512,1792]{1,0:T(8,128)(2,1)S(1)}, bf16[512,1792]{1,0:T(8,128)(2,1)S(1)}, u32[]{:S(2)}, u32[]{:S(2)}) %collective-permute-start.3) | collective-permute-done | bytes 1835040 | tf_op jit(solution)/shard_map/ppermute | solution.py:20
  123.2 1.9 collective-permute-done.4.refs_2_
  125.1 1.5 collective-permute-start.5
  126.6 0.1 collective-permute-start.7
  126.7 34.3 %collective-permute-done.15.refs_1_ = bf16[512,1792]{1,0:T(8,128)(2,1)} collective-permute-done((bf16[512,1792]{1,0:T(8,128)(2,1)S(1)}, bf16[512,1792]{1,0:T(8,128)(2,1)}, u32[]{:S(2)}, u32[]{:S(2)}) %collective-permute-start.15) | collective-permute-done | bytes 1835040 | tf_op jit(solution)/shard_map/ppermute | solution.py:20
  161.0 3.6 collective-permute-done.16.refs_2_
  164.6 1.5 collective-permute-start.17
  166.1 0.1 collective-permute-start.19
  166.1 37.7 %collective-permute-done.5.refs_3_ = bf16[512,1792]{1,0:T(8,128)(2,1)} collective-permute-done((bf16[512,1792]{1,0:T(8,128)(2,1)S(1)}, bf16[512,1792]{1,0:T(8,128)(2,1)}, u32[]{:S(2)}, u32[]{:S(2)}) %collective-permute-start.5) | collective-permute-done | bytes 1835040 | tf_op jit(solution)/shard_map/ppermute | solution.py:20
  203.9 1.6 collective-permute-start.22
  205.5 0.3 collective-permute-start.9
  205.7 37.5 %collective-permute-done.17.refs_3_ = bf16[512,1792]{1,0:T(8,128)(2,1)} collective-permute-done((bf16[512,1792]{1,0:T(8,128)(2,1)}, bf16[512,1792]{1,0:T(8,128)(2,1)}, u32[]{:S(2)}, u32[]{:S(2)}) %collective-permute-start.17) | collective-permute-done | bytes 1835040 | tf_op jit(solution)/shard_map/ppermute | solution.py:20
  243.2 4.7 %fusion.20 = (bf16[256,4096]{1,0:T(8,128)(2,1)}, bf16[256,4096]{1,0:T(8,128)(2,1)}) fusion(bf16[512,4096]{1,0:T(8,128)(2,1)} %all-gather.3.cloned.1.call-done), kind=kLoop, calls=%fused_computation.37 | loop fusion | bytes 8388608 | tf_op jit(solution)/shard_map/slice | solution.py:339
  248.0 0.3 collective-permute-start
  248.3 0.3 collective-permute-start.12
  248.5 31.8 %collective-permute-done.22.refs_4_ = bf16[1792,512]{1,0:T(8,128)(2,1)} collective-permute-done((bf16[1792,512]{1,0:T(8,128)(2,1)}, bf16[1792,512]{1,0:T(8,128)(2,1)}, u32[]{:S(2)}, u32[]{:S(2)}) %collective-permute-start.22) | collective-permute-done | bytes 1835040 | tf_op jit(solution)/shard_map/ppermute | solution.py:20
  280.4 0.5 collective-permute-start.14
  280.9 1.2 constant_dynamic-slice_fusion.3.proj_ref
  282.1 0.6 collective-permute-start.1
  282.7 2.5 constant_dynamic-update-slice_fusion.1
  285.1 11.7 %collective-permute-done = bf16[256,4096]{1,0:T(8,128)(2,1)} collective-permute-done((bf16[256,4096]{1,0:T(8,128)(2,1)}, bf16[256,4096]{1,0:T(8,128)(2,1)}, u32[]{:S(2)}, u32[]{:S(2)}) %collective-permute-start) | collective-permute-done | bytes 2097184 | tf_op jit(solution)/shard_map/ppermute | solution.py:20
  296.8 1.7 constant_dynamic-update-slice_fusion.x_ref
  298.6 2.1 fusion.9
  300.6 0.6 copy-done.2
  301.2 17.8 %shard_map.86.refs_2_ = f32[768,1792]{1,0:T(8,128)} custom-call(s32[1]{0:T(128)} %bitcast.1.place_ref, bf16[768,4096]{1,0:T(8,128)(2,1)} %copy-done.2, bf16[512,1792]{1,0:T(8,128)(2,1)} %copy-done.6, bf16[512,1792]{1,0:T(8,128)(2,1)} %copy-done.8, bf16[512,1792]{1,0:T(8,128)(2,1)} %copy-done.9, bf16[512,1792]{1,0:T(8,128)(2,1)} %collective-permute-done.5.refs_3_, ...), custom_call_target="tpu_custom_call" | custom-call | tf_op jit(solution)/shard_map/pallas_call | solution.py:52
  319.0 17.7 %shard_map.88.refs_0_ = f32[768,1792]{1,0:T(8,128)} custom-call(s32[1]{0:T(128)} %bitcast.1.place_ref, bf16[768,4096]{1,0:T(8,128)(2,1)} %copy-done.2, bf16[512,1792]{1,0:T(8,128)(2,1)} %copy-done.7, bf16[512,1792]{1,0:T(8,128)(2,1)} %collective-permute-done.15.refs_1_, bf16[512,1792]{1,0:T(8,128)(2,1)} %collective-permute-done.16.refs_2_, ...), custom_call_target="tpu_custom_call" | custom-call | tf_op jit(solution)/shard_map/pallas_call | solution.py:52
  336.8 18.1 %shard_map.87.part_ref = f32[1024,1792]{1,0:T(8,128)} custom-call(s32[1]{0:T(128)} %bitcast.1.place_ref, bf16[512,8192]{1,0:T(8,128)(2,1)} %all-gather.5.cloned.1.call-done.y_ref, bf16[1792,512]{1,0:T(8,128)(2,1)} %get-tuple-element.29.refs_0_, bf16[1792,512]{1,0:T(8,128)(2,1)} %collective-permute-done.10.refs_1_, ...), custom_call_target="tpu_custom_call" | custom-call | tf_op jit(solution)/shard_map/pallas_call | solution.py:92
  354.9 4.4 fusion
  359.3 0.6 copy-done.3
  359.9 1.7 fusion.2
  361.6 1.4 copy-done.4
  363.0 11.3 %shard_map.90.refs_3_ = f32[256,1792]{1,0:T(8,128)} custom-call(s32[1]{0:T(128)} %bitcast.1.place_ref, bf16[256,4096]{1,0:T(8,128)(2,1)} %copy-done.4, bf16[512,1792]{1,0:T(8,128)(2,1)} %copy-done.6, bf16[512,1792]{1,0:T(8,128)(2,1)} %copy-done.8, bf16[512,1792]{1,0:T(8,128)(2,1)} %copy-done.9, bf16[512,1792]{1,0:T(8,128)(2,1)} %collective-permute-done.5.refs_3_, ...), custom_call_target="tpu_custom_call" | custom-call | tf_op jit(solution)/shard_map/pallas_call | solution.py:52
  374.3 11.5 %shard_map.89.refs_1_ = f32[256,1792]{1,0:T(8,128)} custom-call(s32[1]{0:T(128)} %bitcast.1.place_ref, bf16[256,4096]{1,0:T(8,128)(2,1)} %copy-done.4, bf16[512,1792]{1,0:T(8,128)(2,1)} %copy-done.7, bf16[512,1792]{1,0:T(8,128)(2,1)} %collective-permute-done.15.refs_1_, bf16[512,1792]{1,0:T(8,128)(2,1)} %collective-permute-done.16.refs_2_, ...), custom_call_target="tpu_custom_call" | custom-call | tf_op jit(solution)/shard_map/pallas_call | solution.py:52
  385.8 0.8 fusion.7
  386.6 0.1 copy-done.19
  386.8 18.3 %shard_map.91 = (f32[1024,128]{1,0:T(8,128)}, f32[1024,128]{1,0:T(8,128)}) custom-call(s32[1]{0:T(128)} %bitcast.1.place_ref, bf16[512,8192]{1,0:T(8,128)(2,1)} %all-gather.5.cloned.1.call-done.y_ref, f32[1024,1792]{1,0:T(8,128)} %shard_map.87.part_ref, bf16[1792,384]{1,0:T(8,128)(2,1)} %constant_dynamic-slice_fusion.3.proj_ref, ...), custom_call_target="tpu_custom_call" | custom-call | tf_op jit(solution)/shard_map/pallas_call | solution.py:137
  405.1 1.5 fusion.14
  406.5 1.5 fusion.4
  408.0 0.7 maximum_bitcast_fusion.1.part_ref
  408.7 16.6 %shard_map.92 = (f32[4,2,2,1024]{3,2,1,0:T(2,128)}, f32[4,1,2,1024]{3,2,1,0:T(2,128)}) custom-call(f32[8,2,1024]{2,1,0:T(2,128)} %maximum_bitcast_fusion.1.part_ref), custom_call_target="tpu_custom_call" | custom-call | tf_op jit(solution)/shard_map/pallas_call | solution.py:262
  425.3 0.9 copy.9
  426.2 0.7 copy.11
  426.9 0.8 copy.10
  427.7 0.6 reshape.77.right_ref
  428.3 6.8 %shard_map.93 = f32[2048,1024]{1,0:T(8,128)} custom-call(f32[8,2048]{1,0:T(8,128)} %bitcast.26, f32[8,1024]{1,0:T(8,128)} %reshape.77.right_ref), custom_call_target="tpu_custom_call" | custom-call | tf_op jit(solution)/shard_map/pallas_call | solution.py:304
  435.1 1.4 constant_dynamic-slice_fusion
  (62 shorter events, 0.2 us)
Async XLA Ops:
  7.2 273.7 %copy-start = (bf16[3584,384]{1,0:T(8,128)(2,1)S(1)}, bf16[3584,384]{1,0:T(8,128)(2,1)}, u32[]{:S(2)}) copy-start(bf16[3584,384]{1,0:T(8,128)(2,1)} %param.13) | copy-start | bytes 8257540
  7.2 236.1 %all-gather.3.cloned.1.call-start = ((), (), s32[]{:S(2)}) async-start(), calls=%async_computation | async-start | bytes 5242880 | tf_op jit(solution)/shard_map/all_gather | solution.py:333
  7.9 328.8 %all-gather.5.cloned.1.call-start = ((), (), s32[]{:S(2)}) async-start(), calls=%async_computation.1 | async-start | bytes 10485760 | tf_op jit(solution)/shard_map/all_gather | solution.py:335
  8.0 26.4 %collective-permute-start.2 = (bf16[128,4096]{1,0:T(8,128)(2,1)}, bf16[128,4096]{1,0:T(8,128)(2,1)S(1)}, u32[]{:S(2)}, u32[]{:S(2)}) collective-permute-start(bf16[128,4096]{1,0:T(8,128)(2,1)} %param.8), channel_id=1, source_target_pairs={{0,16},{4,20},{8,24},{12,28},{16,0},{20,4},{24,8},{28,12},{1,17},{... | collective-permute-start | bytes 3145736 | tf_op jit(solution)/shard_map/ppermute | solution.py:20
  37.2 7.0 %copy-start.16 = (bf16[512,3584]{1,0:T(8,128)(2,1)S(1)}, bf16[512,3584]{1,0:T(8,128)(2,1)}, u32[]{:S(2)}) copy-start(bf16[512,3584]{1,0:T(8,128)(2,1)} %param.10) | copy-start | bytes 11010052
  41.0 43.0 %collective-permute-start.10 = (bf16[1792,512]{1,0:T(8,128)(2,1)S(1)}, bf16[1792,512]{1,0:T(8,128)(2,1)}, u32[]{:S(2)}, u32[]{:S(2)}) collective-permute-start(bf16[1792,512]{1,0:T(8,128)(2,1)S(1)} %get-tuple-element.28), channel_id=1, source_target_pairs={{0,16},{4,20},{8,24},{12,28},{16,0},{20,4},{24,8},{28,12},{1,17},{... | collective-permute-start | bytes 5505032 | tf_op jit(solution)/shard_map/ppermute | solution.py:20
  42.7 2.6 copy-start.17
  42.7 43.2 %collective-permute-start.11 = (bf16[1792,512]{1,0:T(8,128)(2,1)}, bf16[1792,512]{1,0:T(8,128)(2,1)}, u32[]{:S(2)}, u32[]{:S(2)}) collective-permute-start(bf16[1792,512]{1,0:T(8,128)(2,1)} %get-tuple-element.29.refs_0_), channel_id=1, source_target_pairs={{0,8},{4,12},{8,0},{12,4},{16,24},{20,28},{24,16},{28,20},{1,9},{5... | collective-permute-start | bytes 5505032 | tf_op jit(solution)/shard_map/ppermute | solution.py:20
  44.4 1.3 copy-start.6
  44.5 78.7 %collective-permute-start.3 = (bf16[512,1792]{1,0:T(8,128)(2,1)S(1)}, bf16[512,1792]{1,0:T(8,128)(2,1)S(1)}, u32[]{:S(2)}, u32[]{:S(2)}) collective-permute-start(bf16[512,1792]{1,0:T(8,128)(2,1)S(1)} %get-tuple-element.30), channel_id=1, source_target_pairs={{0,16},{4,20},{8,24},{12,28},{16,0},{20,4},{24,8},{28,12},{1,17},{... | collective-permute-start | bytes 5505032 | tf_op jit(solution)/shard_map/ppermute | solution.py:20
  45.0 80.1 %collective-permute-start.4 = (bf16[512,1792]{1,0:T(8,128)(2,1)S(1)}, bf16[512,1792]{1,0:T(8,128)(2,1)S(1)}, u32[]{:S(2)}, u32[]{:S(2)}) collective-permute-start(bf16[512,1792]{1,0:T(8,128)(2,1)S(1)} %get-tuple-element.31.refs_0_), channel_id=1, source_target_pairs={{0,8},{4,12},{8,0},{12,4},{16,24},{20,28},{24,16},{28,20},{1,9},{5... | collective-permute-start | bytes 5505032 | tf_op jit(solution)/shard_map/ppermute | solution.py:20
  45.3 81.3 %collective-permute-start.6 = (bf16[512,1792]{1,0:T(8,128)(2,1)S(1)}, bf16[512,1792]{1,0:T(8,128)(2,1)S(1)}, u32[]{:S(2)}, u32[]{:S(2)}) collective-permute-start(bf16[512,1792]{1,0:T(8,128)(2,1)S(1)} %get-tuple-element.31.refs_0_), channel_id=1, source_target_pairs={{0,4},{4,0},{8,12},{12,8},{16,20},{20,16},{24,28},{28,24},{1,5},{5... | collective-permute-start | bytes 5505032 | tf_op jit(solution)/shard_map/ppermute | solution.py:20
  45.7 80.9 %copy-start.7 = (bf16[512,1792]{1,0:T(8,128)(2,1)}, bf16[512,1792]{1,0:T(8,128)(2,1)S(1)}, u32[]{:S(2)}) copy-start(bf16[512,1792]{1,0:T(8,128)(2,1)S(1)} %get-tuple-element.27.refs_0_) | copy-start | bytes 5505028
  84.0 77.0 %collective-permute-start.15 = (bf16[512,1792]{1,0:T(8,128)(2,1)S(1)}, bf16[512,1792]{1,0:T(8,128)(2,1)}, u32[]{:S(2)}, u32[]{:S(2)}) collective-permute-start(bf16[512,1792]{1,0:T(8,128)(2,1)S(1)} %get-tuple-element.26), channel_id=1, source_target_pairs={{0,16},{4,20},{8,24},{12,28},{16,0},{20,4},{24,8},{28,12},{1,17},{... | collective-permute-start | bytes 5505032 | tf_op jit(solution)/shard_map/ppermute | solution.py:20
  85.9 78.6 %collective-permute-start.16 = (bf16[512,1792]{1,0:T(8,128)(2,1)S(1)}, bf16[512,1792]{1,0:T(8,128)(2,1)}, u32[]{:S(2)}, u32[]{:S(2)}) collective-permute-start(bf16[512,1792]{1,0:T(8,128)(2,1)S(1)} %get-tuple-element.27.refs_0_), channel_id=1, source_target_pairs={{0,8},{4,12},{8,0},{12,4},{16,24},{20,28},{24,16},{28,20},{1,9},{5... | collective-permute-start | bytes 5505032 | tf_op jit(solution)/shard_map/ppermute | solution.py:20
  123.2 42.9 %copy-start.8 = (bf16[512,1792]{1,0:T(8,128)(2,1)}, bf16[512,1792]{1,0:T(8,128)(2,1)S(1)}, u32[]{:S(2)}) copy-start(bf16[512,1792]{1,0:T(8,128)(2,1)S(1)} %collective-permute-done.3.refs_1_) | copy-start | bytes 5505028
  123.2 42.9 %collective-permute-start.18 = (bf16[512,1792]{1,0:T(8,128)(2,1)S(1)}, bf16[512,1792]{1,0:T(8,128)(2,1)S(1)}, u32[]{:S(2)}, u32[]{:S(2)}) collective-permute-start(bf16[512,1792]{1,0:T(8,128)(2,1)S(1)} %get-tuple-element.27.refs_0_), channel_id=1, source_target_pairs={{0,4},{4,0},{8,12},{12,8},{16,20},{20,16},{24,28},{28,24},{1,5},{5... | collective-permute-start | bytes 5505032 | tf_op jit(solution)/shard_map/ppermute | solution.py:20
  125.1 78.8 %copy-start.9 = (bf16[512,1792]{1,0:T(8,128)(2,1)}, bf16[512,1792]{1,0:T(8,128)(2,1)S(1)}, u32[]{:S(2)}) copy-start(bf16[512,1792]{1,0:T(8,128)(2,1)S(1)} %collective-permute-done.4.refs_2_) | copy-start | bytes 5505028
  125.1 78.8 %collective-permute-start.5 = (bf16[512,1792]{1,0:T(8,128)(2,1)S(1)}, bf16[512,1792]{1,0:T(8,128)(2,1)}, u32[]{:S(2)}, u32[]{:S(2)}) collective-permute-start(bf16[512,1792]{1,0:T(8,128)(2,1)S(1)} %collective-permute-done.3.refs_1_), channel_id=1, source_target_pairs={{0,8},{4,12},{8,0},{12,4},{16,24},{20,28},{24,16},{28,20},{1,9},{5... | collective-permute-start | bytes 5505032 | tf_op jit(solution)/shard_map/ppermute | solution.py:20
  126.6 78.8 %copy-start.10 = (bf16[512,1792]{1,0:T(8,128)(2,1)}, bf16[512,1792]{1,0:T(8,128)(2,1)S(1)}, u32[]{:S(2)}) copy-start(bf16[512,1792]{1,0:T(8,128)(2,1)S(1)} %collective-permute-done.6.refs_4_) | copy-start | bytes 5505028
  126.6 77.3 %collective-permute-start.7 = (bf16[512,1792]{1,0:T(8,128)(2,1)S(1)}, bf16[512,1792]{1,0:T(8,128)(2,1)S(1)}, u32[]{:S(2)}, u32[]{:S(2)}) collective-permute-start(bf16[512,1792]{1,0:T(8,128)(2,1)S(1)} %collective-permute-done.3.refs_1_), channel_id=1, source_target_pairs={{0,4},{4,0},{8,12},{12,8},{16,20},{20,16},{24,28},{28,24},{1,5},{5... | collective-permute-start | bytes 5505032 | tf_op jit(solution)/shard_map/ppermute | solution.py:20
  161.0 44.5 %collective-permute-start.8 = (bf16[512,1792]{1,0:T(8,128)(2,1)S(1)}, bf16[512,1792]{1,0:T(8,128)(2,1)S(1)}, u32[]{:S(2)}, u32[]{:S(2)}) collective-permute-start(bf16[512,1792]{1,0:T(8,128)(2,1)S(1)} %collective-permute-done.4.refs_2_), channel_id=1, source_target_pairs={{0,4},{4,0},{8,12},{12,8},{16,20},{20,16},{24,28},{28,24},{1,5},{5... | collective-permute-start | bytes 5505032 | tf_op jit(solution)/shard_map/ppermute | solution.py:20
  164.6 78.6 %collective-permute-start.17 = (bf16[512,1792]{1,0:T(8,128)(2,1)}, bf16[512,1792]{1,0:T(8,128)(2,1)}, u32[]{:S(2)}, u32[]{:S(2)}) collective-permute-start(bf16[512,1792]{1,0:T(8,128)(2,1)} %collective-permute-done.15.refs_1_), channel_id=1, source_target_pairs={{0,8},{4,12},{8,0},{12,4},{16,24},{20,28},{24,16},{28,20},{1,9},{5... | collective-permute-start | bytes 5505032 | tf_op jit(solution)/shard_map/ppermute | solution.py:20
  166.1 39.7 %copy-start.11 = (bf16[512,1792]{1,0:T(8,128)(2,1)}, bf16[512,1792]{1,0:T(8,128)(2,1)S(1)}, u32[]{:S(2)}) copy-start(bf16[512,1792]{1,0:T(8,128)(2,1)S(1)} %collective-permute-done.18.refs_4_) | copy-start | bytes 5505028
  166.1 81.9 %collective-permute-start.19 = (bf16[512,1792]{1,0:T(8,128)(2,1)}, bf16[512,1792]{1,0:T(8,128)(2,1)}, u32[]{:S(2)}, u32[]{:S(2)}) collective-permute-start(bf16[512,1792]{1,0:T(8,128)(2,1)} %collective-permute-done.15.refs_1_), channel_id=1, source_target_pairs={{0,4},{4,0},{8,12},{12,8},{16,20},{20,16},{24,28},{28,24},{1,5},{5... | collective-permute-start | bytes 5505032 | tf_op jit(solution)/shard_map/ppermute | solution.py:20
  203.9 44.4 %collective-permute-start.20 = (bf16[512,1792]{1,0:T(8,128)(2,1)}, bf16[512,1792]{1,0:T(8,128)(2,1)}, u32[]{:S(2)}, u32[]{:S(2)}) collective-permute-start(bf16[512,1792]{1,0:T(8,128)(2,1)} %collective-permute-done.16.refs_2_), channel_id=1, source_target_pairs={{0,4},{4,0},{8,12},{12,8},{16,20},{20,16},{24,28},{28,24},{1,5},{5... | collective-permute-start | bytes 5505032 | tf_op jit(solution)/shard_map/ppermute | solution.py:20
  203.9 39.3 %copy-start.12 = (bf16[512,1792]{1,0:T(8,128)(2,1)}, bf16[512,1792]{1,0:T(8,128)(2,1)S(1)}, u32[]{:S(2)}) copy-start(bf16[512,1792]{1,0:T(8,128)(2,1)S(1)} %collective-permute-done.7.refs_5_) | copy-start | bytes 5505028
  203.9 76.5 %collective-permute-start.22 = (bf16[1792,512]{1,0:T(8,128)(2,1)}, bf16[1792,512]{1,0:T(8,128)(2,1)}, u32[]{:S(2)}, u32[]{:S(2)}) collective-permute-start(bf16[1792,512]{1,0:T(8,128)(2,1)} %collective-permute-done.10.refs_1_), channel_id=1, source_target_pairs={{0,8},{4,12},{8,0},{12,4},{16,24},{20,28},{24,16},{28,20},{1,9},{5... | collective-permute-start | bytes 5505032 | tf_op jit(solution)/shard_map/ppermute | solution.py:20
  205.5 37.7 %copy-start.13 = (bf16[512,1792]{1,0:T(8,128)(2,1)}, bf16[512,1792]{1,0:T(8,128)(2,1)S(1)}, u32[]{:S(2)}) copy-start(bf16[512,1792]{1,0:T(8,128)(2,1)S(1)} %collective-permute-done.8.refs_6_) | copy-start | bytes 5505028
  205.5 74.9 %collective-permute-start.9 = (bf16[512,1792]{1,0:T(8,128)(2,1)}, bf16[512,1792]{1,0:T(8,128)(2,1)}, u32[]{:S(2)}, u32[]{:S(2)}) collective-permute-start(bf16[512,1792]{1,0:T(8,128)(2,1)} %collective-permute-done.5.refs_3_), channel_id=1, source_target_pairs={{0,4},{4,0},{8,12},{12,8},{16,20},{20,16},{24,28},{28,24},{1,5},{5... | collective-permute-start | bytes 5505032 | tf_op jit(solution)/shard_map/ppermute | solution.py:20
  243.2 38.9 %collective-permute-start.21 = (bf16[512,1792]{1,0:T(8,128)(2,1)}, bf16[512,1792]{1,0:T(8,128)(2,1)}, u32[]{:S(2)}, u32[]{:S(2)}) collective-permute-start(bf16[512,1792]{1,0:T(8,128)(2,1)} %collective-permute-done.17.refs_3_), channel_id=1, source_target_pairs={{0,4},{4,0},{8,12},{12,8},{16,20},{20,16},{24,28},{28,24},{1,5},{5... | collective-permute-start | bytes 5505032 | tf_op jit(solution)/shard_map/ppermute | solution.py:20
  248.0 48.8 %collective-permute-start = (bf16[256,4096]{1,0:T(8,128)(2,1)}, bf16[256,4096]{1,0:T(8,128)(2,1)}, u32[]{:S(2)}, u32[]{:S(2)}) collective-permute-start(bf16[256,4096]{1,0:T(8,128)(2,1)} %get-tuple-element.24), channel_id=1, source_target_pairs={{0,16},{4,20},{8,24},{12,28},{16,0},{20,4},{24,8},{28,12},{1,17},{... | collective-permute-start | bytes 6291464 | tf_op jit(solution)/shard_map/ppermute | solution.py:20
  248.3 88.4 %collective-permute-start.12 = (bf16[1792,512]{1,0:T(8,128)(2,1)}, bf16[1792,512]{1,0:T(8,128)(2,1)}, u32[]{:S(2)}, u32[]{:S(2)}) collective-permute-start(bf16[1792,512]{1,0:T(8,128)(2,1)} %get-tuple-element.29.refs_0_), channel_id=1, source_target_pairs={{0,4},{4,0},{8,12},{12,8},{16,20},{20,16},{24,28},{28,24},{1,5},{5... | collective-permute-start | bytes 5505032 | tf_op jit(solution)/shard_map/ppermute | solution.py:20
  280.4 56.4 %collective-permute-start.13 = (bf16[1792,512]{1,0:T(8,128)(2,1)}, bf16[1792,512]{1,0:T(8,128)(2,1)}, u32[]{:S(2)}, u32[]{:S(2)}) collective-permute-start(bf16[1792,512]{1,0:T(8,128)(2,1)} %collective-permute-done.10.refs_1_), channel_id=1, source_target_pairs={{0,4},{4,0},{8,12},{12,8},{16,20},{20,16},{24,28},{28,24},{1,5},{5... | collective-permute-start | bytes 5505032 | tf_op jit(solution)/shard_map/ppermute | solution.py:20
  280.4 56.4 %collective-permute-start.14 = (bf16[1792,512]{1,0:T(8,128)(2,1)}, bf16[1792,512]{1,0:T(8,128)(2,1)}, u32[]{:S(2)}, u32[]{:S(2)}) collective-permute-start(bf16[1792,512]{1,0:T(8,128)(2,1)} %collective-permute-done.11.refs_2_), channel_id=1, source_target_pairs={{0,4},{4,0},{8,12},{12,8},{16,20},{20,16},{24,28},{28,24},{1,5},{5... | collective-permute-start | bytes 5505032 | tf_op jit(solution)/shard_map/ppermute | solution.py:20
  282.1 79.5 %collective-permute-start.1 = (bf16[256,4096]{1,0:T(8,128)(2,1)}, bf16[256,4096]{1,0:T(8,128)(2,1)S(1)}, u32[]{:S(2)}, u32[]{:S(2)}) collective-permute-start(bf16[256,4096]{1,0:T(8,128)(2,1)} %get-tuple-element.25), channel_id=1, source_target_pairs={{0,16},{4,20},{8,24},{12,28},{16,0},{20,4},{24,8},{28,12},{1,17},{... | collective-permute-start | bytes 6291464 | tf_op jit(solution)/shard_map/ppermute | solution.py:20
  285.1 13.4 %copy-start.14 = (bf16[4096,128]{1,0:T(8,128)(2,1)S(1)}, bf16[4096,128]{1,0:T(8,128)(2,1)}, u32[]{:S(2)}) copy-start(bf16[4096,128]{1,0:T(8,128)(2,1)} %param.12) | copy-start | bytes 3145732
  296.8 90.0 %collective-permute-start.23 = (bf16[1792,512]{1,0:T(8,128)(2,1)}, bf16[1792,512]{1,0:T(8,128)(2,1)}, u32[]{:S(2)}, u32[]{:S(2)}) collective-permute-start(bf16[1792,512]{1,0:T(8,128)(2,1)} %collective-permute-done.22.refs_4_), channel_id=1, source_target_pairs={{0,4},{4,0},{8,12},{12,8},{16,20},{20,16},{24,28},{28,24},{1,5},{5... | collective-permute-start | bytes 5505032 | tf_op jit(solution)/shard_map/ppermute | solution.py:20
  298.5 2.7 copy-start.2
  301.2 17.8 %copy-start.18 = (f32[768,64]{0,1:T(8,128)}, f32[768,64]{0,1:T(8,128)S(1)}, u32[]{:S(2)}) copy-start(f32[768,64]{0,1:T(8,128)S(1)} %fusion.9) | copy-start | bytes 589828
  336.8 22.5 %copy-start.15 = (bf16[4096,128]{1,0:T(8,128)(2,1)S(1)}, bf16[4096,128]{1,0:T(8,128)(2,1)}, u32[]{:S(2)}) copy-start(bf16[4096,128]{1,0:T(8,128)(2,1)} %param.12) | copy-start | bytes 3145732
  354.9 5.0 %copy-start.3 = (bf16[512,8192]{1,0:T(8,128)(2,1)S(1)}, bf16[512,8192]{1,0:T(8,128)(2,1)}, u32[]{:S(2)}) copy-start(bf16[512,8192]{1,0:T(8,128)(2,1)} %all-gather.5.cloned.1.call-done.y_ref) | copy-start | bytes 25165828
  361.6 1.4 copy-start.4
  374.3 11.5 %copy-start.5 = (bf16[256,4096]{1,0:T(8,128)(2,1)S(1)}, bf16[256,4096]{1,0:T(8,128)(2,1)}, u32[]{:S(2)}) copy-start(bf16[256,4096]{1,0:T(8,128)(2,1)} %copy-done.4) | copy-start | bytes 6291460
  385.8 0.9 copy-start.19
  385.8 0.9 slice-start
  428.3 8.3 %copy-start.1 = (bf16[3584,384]{1,0:T(8,128)(2,1)S(1)}, bf16[3584,384]{1,0:T(8,128)(2,1)}, u32[]{:S(2)}) copy-start(bf16[3584,384]{1,0:T(8,128)(2,1)} %param.13) | copy-start | bytes 8257540
Sparse Core Ops, SparseCore 0:
  9.6 83.4 all-gather.2
  94.6 148.0 all-gather.4
